TPU v7x, 32 devices: a whole 2x2x4 slice. The times are simulated.
32 devices in a mesh: dp: 4 (over y, x), seq: 8 (over z, core).
Axes of the slice: x: 2, y: 2, z: 4, core: 2. Of those that a mesh axis runs over, the one named last changes fastest.
Arguments:
- inputs: bfloat16 [8, 1536, 768], P('dp', 'seq'), may hold values from -6 to 6
- segments: int32 [8, 1536], P('dp'), may hold values from 0 to 5, never falling along the last dimension, each value on 1 to 1152 neighbouring positions
- rand_blocks: int32 [8, 24, 12, 3], P('dp'), may hold values from 0 to 23, as said below
- w_qkv: bfloat16 [768, 2304], P('dp'), may hold values from -0.21875 to 0.21875
- w_out: bfloat16 [768, 768], P('dp'), may hold values from -1.75 to 1.75
- w_up: bfloat16 [768, 3072], P('dp'), may hold values from -0.21875 to 0.21875
- w_down: bfloat16 [3072, 768], P('dp'), may hold values from -0.109375 to 0.109375
- norm_gain: float32 [2, 768], replicated, may hold values from 0.5 to 1.5
- norm_bias: float32 [2, 768], replicated, may hold values from -3 to 3
- out_grad: bfloat16 [8, 1536, 768], P('dp', 'seq'), may hold values from -6 to 6
Outputs:
- output: bfloat16 [8, 1536, 768], P('dp', 'seq')
- input_grad: float32 [8, 1536, 768], P('dp', 'seq')
- w_qkv_grad: float32 [768, 2304], P(('dp', 'seq'))
- w_out_grad: float32 [768, 768], P(('dp', 'seq'))
- w_up_grad: float32 [768, 3072], P(('dp', 'seq'))
- w_down_grad: float32 [3072, 768], P(('dp', 'seq'))
- norm_gain_grad: float32 [2, 768], P(None, ('dp', 'seq'))
- norm_bias_grad: float32 [2, 768], P(None, ('dp', 'seq'))
Inputs may be any that keep to these rules, and one draw needn't show every extreme that they name: `rand_blocks`: for every sequence and every index t of seq, among the 108 entries of the query blocks t * 3 .. (t + 1) * 3 - 1, at most 14 name key blocks held by one index of seq (key block // 3), and some index is named exactly 14 times.
All inputs are finite; a program needn't handle non-finite values.
Results may differ from a plain program's by a relative error of at most 0.013.
Values may be sent and summed in bfloat16 or wider, within the bound.
A program may use at most 192 MiB of HBM per device.

v0:
```python
import jax
import jax.numpy as jnp
import numpy as np
from jax import lax
from jax.sharding import PartitionSpec as P

H = 12
HEAD = 64
BLOCK = 64
R = 3
MICRO = 2


norm_eps = 1e-05
masked_score = -1e30
root_half = 0.7071067811865476
inv_root_two_pi = 0.3989422804014327


def padded(cells, sides, width):
    for axis, dim in sides:
        count = lax.axis_size(axis)
        ends = count - 1
        head = lax.slice_in_dim(cells, 0, width, axis=dim)
        tail = lax.slice_in_dim(cells, cells.shape[dim] - width, cells.shape[dim], axis=dim)
        cells = jnp.concatenate(
            [
                lax.ppermute(tail, axis, [(i, (i + 1) % count) for i in range(ends)]),
                cells,
                lax.ppermute(head, axis, [((i + 1) % count, i) for i in range(ends)]),
            ],
            axis=dim,
        )
    return cells


def from_root(x, axis, root):
    mine = lax.axis_index(axis) == root
    return lax.psum(jnp.where(mine, x, jnp.zeros_like(x)), axis)


def merged(x, axis, combine):
    everything = jax.tree.map(lambda part: lax.all_gather(part, axis), x)
    initial = jax.tree.map(lambda part: part[0], everything)

    def step(k, so_far):
        return combine(so_far, jax.tree.map(lambda part: part[k], everything))

    return lax.fori_loop(1, lax.axis_size(axis), step, initial)


def product(left_side, right_side):
    return jnp.dot(left_side, right_side, preferred_element_type=jnp.float32)


def product_tn(left_side, right_side):
    return lax.dot_general(
        left_side, right_side, (((0,), (0,)), ((), ())), preferred_element_type=jnp.float32
    )


def product_nt(left_side, right_side):
    return lax.dot_general(
        left_side, right_side, (((1,), (1,)), ((), ())), preferred_element_type=jnp.float32
    )


def gelu_value(pre_act):
    return 0.5 * pre_act * (1.0 + lax.erf(pre_act * root_half))


def gelu_slope(pre_act):
    return (
        0.5 * (1.0 + lax.erf(pre_act * root_half))
        + pre_act * jnp.exp(-0.5 * pre_act * pre_act) * inv_root_two_pi
    )


def norm_forward(residual, gain_row, shift_row):
    mean_row = jnp.mean(residual, axis=-1, keepdims=True)
    centred = residual - mean_row
    variance = jnp.mean(centred * centred, axis=-1, keepdims=True)
    inv_std = lax.rsqrt(variance + norm_eps)
    normed = centred * inv_std
    return (normed * gain_row + shift_row, normed, inv_std)


def norm_backward(grad_rows, normed, inv_std, gain_row):
    scaled = grad_rows * gain_row
    back_rows = inv_std * (
        scaled
        - jnp.mean(scaled, axis=-1, keepdims=True)
        - normed * jnp.mean(scaled * normed, axis=-1, keepdims=True)
    )
    return (back_rows, jnp.sum(grad_rows * normed, axis=0), jnp.sum(grad_rows, axis=0))


def merge_stats(first_pair, second_pair):
    joint_max = jnp.maximum(first_pair[0], second_pair[0])
    joint_sum = first_pair[1] * jnp.exp(first_pair[0] - joint_max) + second_pair[1] * jnp.exp(
        second_pair[0] - joint_max
    )
    return (joint_max, joint_sum)


def local_scores(query_heads, shared_keys, random_keys, shared_ok, random_ok, scale_factor):
    part_shared = jnp.einsum(
        "sbqhd,sbkhd->sbhqk", query_heads, shared_keys, preferred_element_type=jnp.float32
    )
    part_random = jnp.einsum(
        "sbqhd,sbhkd->sbhqk", query_heads, random_keys, preferred_element_type=jnp.float32
    )
    scores = jnp.concatenate([part_shared, part_random], axis=4) * scale_factor
    allowed = jnp.concatenate(
        [jnp.broadcast_to(shared_ok[:, :, None], part_shared.shape), random_ok], axis=4
    )
    return jnp.where(allowed, scores, masked_score)


def per_device(
    inputs, segments, rand_blocks, w_qkv, w_out, w_up, w_down, norm_gain, norm_bias, out_grad
):
    seq_total, tok_dev, features = inputs.shape
    devices = lax.axis_size("seq")
    my_index = lax.axis_index("seq")
    blocks_dev = tok_dev // BLOCK
    blocks_all = blocks_dev * devices
    entries = blocks_dev * H * R
    capacity = max(2, entries // devices + 1)
    per_micro = seq_total // MICRO
    glob_rows = 2 * BLOCK
    shared_count = 5 * BLOCK
    scale_factor = HEAD ** (-0.5)
    token_rows = per_micro * tok_dev
    owner_flag = (my_index == 0).astype(jnp.float32)
    row_global = my_index * tok_dev + jnp.arange(tok_dev, dtype=jnp.int32) < glob_rows
    window_index = np.arange(blocks_dev)[:, None] + np.arange(3)[None, :]
    win_blocks = (
        my_index * blocks_dev
        + jnp.arange(blocks_dev, dtype=jnp.int32)[:, None]
        + jnp.arange(-1, 2, dtype=jnp.int32)[None, :]
    )
    win_inside = (win_blocks >= 0) & (win_blocks < blocks_all)
    win_clipped = jnp.clip(win_blocks, 0, blocks_all - 1)
    entry_heads = jnp.arange(entries, dtype=jnp.int32) // R % H
    slot_ids = jnp.arange(capacity, dtype=jnp.int32)
    earlier = jnp.arange(entries)[None, :] < jnp.arange(entries)[:, None]
    seq_ids = jnp.arange(per_micro, dtype=jnp.int32)
    grad_qkv_w = jnp.zeros((features, 3 * features), jnp.float32)
    grad_out_w = jnp.zeros((features, features), jnp.float32)
    grad_up_w = jnp.zeros((features, w_up.shape[1]), jnp.float32)
    grad_down_w = jnp.zeros((w_down.shape[0] * lax.axis_size("dp"), features), jnp.float32)
    gain_acc = jnp.zeros((2, features), jnp.float32)
    shift_acc = jnp.zeros((2, features), jnp.float32)
    output_parts = []
    input_parts = []
    for micro_step in range(MICRO):
        start_seq = micro_step * per_micro
        tokens_in = inputs[start_seq : start_seq + per_micro]
        seg_micro = segments[start_seq : start_seq + per_micro]
        rand_micro = rand_blocks[start_seq : start_seq + per_micro]
        cotangent = out_grad[start_seq : start_seq + per_micro]
        full_qkv, full_out, full_up, full_down = (
            lax.all_gather(w_qkv, "dp", axis=0, tiled=True),
            lax.all_gather(w_out, "dp", axis=0, tiled=True),
            lax.all_gather(w_up, "dp", axis=0, tiled=True),
            lax.all_gather(w_down, "dp", axis=0, tiled=True),
        )
        tokens_flat = tokens_in.reshape(token_rows, features)
        qkv_rows = (
            product(tokens_flat, full_qkv)
            .astype(jnp.bfloat16)
            .reshape(per_micro, tok_dev, 3 * features)
        )
        queries = qkv_rows[..., :features]
        keyvals = qkv_rows[..., features:]
        extended = padded(keyvals, (("seq", 1),), BLOCK)
        global_block = from_root(qkv_rows[:, :glob_rows], "seq", 0)
        requests = rand_micro.reshape(per_micro, devices, entries)
        owners = requests // blocks_dev
        local_block = requests % blocks_dev
        same_owner = owners[:, :, :, None] == owners[:, :, None, :]
        slot_rank = jnp.sum(same_owner & earlier[None, None], axis=3)
        slot_hit = ((owners == my_index)[..., None] & (slot_rank[..., None] == slot_ids)).astype(
            jnp.int32
        )
        slot_live = jnp.sum(slot_hit, axis=2)
        slot_piece = jnp.sum(slot_hit * (local_block * H + entry_heads)[..., None], axis=2)
        piece_index = jnp.transpose(slot_piece, (1, 2, 0))
        live_mask = jnp.transpose(slot_live, (1, 2, 0))
        pieces = (
            keyvals.reshape(per_micro, blocks_dev, BLOCK, 2, H, HEAD)
            .transpose(0, 1, 4, 2, 3, 5)
            .reshape(per_micro, blocks_dev * H, BLOCK, 2 * HEAD)
        )
        outgoing = pieces[seq_ids[None, None, :], piece_index]
        outgoing = jnp.where(live_mask[..., None, None] > 0, outgoing, jnp.zeros((), jnp.bfloat16))
        outgoing = outgoing.reshape(devices * capacity, per_micro, BLOCK, 2 * HEAD)
        incoming = lax.all_to_all(outgoing, "seq", split_axis=0, concat_axis=0, tiled=True)
        my_owner = jnp.take(owners, my_index, axis=1)
        my_rank = jnp.take(slot_rank, my_index, axis=1)
        my_request = jnp.take(requests, my_index, axis=1)
        positions = my_owner * capacity + my_rank
        fetched = incoming[positions, seq_ids[:, None]].reshape(
            per_micro, blocks_dev, H, R, BLOCK, 2, HEAD
        )
        random_keys = fetched[..., 0, :].reshape(per_micro, blocks_dev, H, R * BLOCK, HEAD)
        random_vals = fetched[..., 1, :].reshape(per_micro, blocks_dev, H, R * BLOCK, HEAD)
        seg_blocks = seg_micro.reshape(per_micro, blocks_all, BLOCK)
        query_seg = lax.dynamic_slice_in_dim(seg_micro, my_index * tok_dev, tok_dev, 1).reshape(
            per_micro, blocks_dev, BLOCK
        )
        window_seg = seg_blocks[:, win_clipped].reshape(per_micro, blocks_dev, 3 * BLOCK)
        window_ok = (query_seg[..., :, None] == window_seg[:, :, None, :]) & jnp.repeat(
            win_inside, BLOCK, axis=1
        )[None, :, None, :]
        shared_ok = jnp.concatenate(
            [window_ok, jnp.ones((per_micro, blocks_dev, BLOCK, glob_rows), bool)], axis=3
        )
        random_seg = seg_blocks[seq_ids[:, None], my_request].reshape(
            per_micro, blocks_dev, H, R * BLOCK
        )
        random_ok = query_seg[:, :, None, :, None] == random_seg[:, :, :, None, :]
        ext_blocks = extended.reshape(per_micro, blocks_dev + 2, BLOCK, 2 * features)
        window_kv = ext_blocks[:, window_index].reshape(
            per_micro, blocks_dev, 3 * BLOCK, 2 * features
        )
        glob_kv = jnp.broadcast_to(
            global_block[:, None, :, features:], (per_micro, blocks_dev, glob_rows, 2 * features)
        )
        shared_kv = jnp.concatenate([window_kv, glob_kv], axis=2)
        shared_keys = shared_kv[..., :features].reshape(
            per_micro, blocks_dev, shared_count, H, HEAD
        )
        shared_vals = shared_kv[..., features:].reshape(
            per_micro, blocks_dev, shared_count, H, HEAD
        )
        query_heads = queries.reshape(per_micro, blocks_dev, BLOCK, H, HEAD)
        scores = local_scores(
            query_heads, shared_keys, random_keys, shared_ok, random_ok, scale_factor
        )
        row_max = jnp.max(scores, axis=4, keepdims=True)
        exp_terms = jnp.exp(scores - row_max)
        row_sum = jnp.sum(exp_terms, axis=4, keepdims=True)
        local_probs = exp_terms / row_sum
        log_norm = row_max + jnp.log(row_sum)
        local_weights = local_probs.astype(jnp.bfloat16)
        local_att = jnp.einsum(
            "sbhqk,sbkhd->sbqhd",
            local_weights[..., :shared_count],
            shared_vals,
            preferred_element_type=jnp.float32,
        )
        local_att = local_att + jnp.einsum(
            "sbhqk,sbhkd->sbqhd",
            local_weights[..., shared_count:],
            random_vals,
            preferred_element_type=jnp.float32,
        )
        local_att = local_att.reshape(per_micro, tok_dev, features)
        glob_query = global_block[..., :features].reshape(per_micro, glob_rows, H, HEAD)
        local_keys = keyvals[..., :features].reshape(per_micro, tok_dev, H, HEAD)
        local_vals = keyvals[..., features:].reshape(per_micro, tok_dev, H, HEAD)
        glob_scores = (
            jnp.einsum(
                "sqhd,skhd->shqk", glob_query, local_keys, preferred_element_type=jnp.float32
            )
            * scale_factor
        )
        part_max = jnp.max(glob_scores, axis=3)
        part_sum = jnp.sum(jnp.exp(glob_scores - part_max[..., None]), axis=3)
        glob_max, glob_sum = merged((part_max, part_sum), "seq", merge_stats)
        glob_lse = glob_max + jnp.log(glob_sum)
        glob_probs = jnp.exp(glob_scores - glob_lse[..., None])
        glob_weights = glob_probs.astype(jnp.bfloat16)
        glob_part = jnp.einsum(
            "shqk,skhd->sqhd", glob_weights, local_vals, preferred_element_type=jnp.float32
        ).reshape(per_micro, glob_rows, features)
        glob_out = lax.psum(glob_part, "seq")
        glob_full = jnp.concatenate(
            [glob_out, jnp.zeros((per_micro, tok_dev - glob_rows, features), jnp.float32)], axis=1
        )
        attention = jnp.where(row_global[None, :, None], glob_full, local_att).astype(jnp.bfloat16)
        att_flat = attention.reshape(token_rows, features)
        resid_one = tokens_flat.astype(jnp.float32) + product(att_flat, full_out)
        hidden_one, normed_one, inv_one = norm_forward(resid_one, norm_gain[0], norm_bias[0])
        hidden_low = hidden_one.astype(jnp.bfloat16)
        pre_act = product(hidden_low, full_up)
        activated = gelu_value(pre_act).astype(jnp.bfloat16)
        resid_two = hidden_one + product(activated, full_down)
        result, normed_two, inv_two = norm_forward(resid_two, norm_gain[1], norm_bias[1])
        output_parts.append(result.astype(jnp.bfloat16).reshape(per_micro, tok_dev, features))
        grad_rows = cotangent.reshape(token_rows, features).astype(jnp.float32)
        grad_resid_two, gain_two, shift_two = norm_backward(
            grad_rows, normed_two, inv_two, norm_gain[1]
        )
        grad_branch = grad_resid_two.astype(jnp.bfloat16)
        grad_down_w = grad_down_w + product_tn(activated, grad_branch)
        grad_pre = (product_nt(grad_branch, full_down) * gelu_slope(pre_act)).astype(jnp.bfloat16)
        grad_up_w = grad_up_w + product_tn(hidden_low, grad_pre)
        grad_hidden = grad_resid_two + product_nt(grad_pre, full_up)
        grad_resid_one, gain_one, shift_one = norm_backward(
            grad_hidden, normed_one, inv_one, norm_gain[0]
        )
        grad_mix = grad_resid_one.astype(jnp.bfloat16)
        grad_out_w = grad_out_w + product_tn(att_flat, grad_mix)
        grad_att = (
            product_nt(grad_mix, full_out)
            .astype(jnp.bfloat16)
            .reshape(per_micro, tok_dev, features)
        )
        gain_acc = gain_acc + jnp.stack([gain_one, gain_two])
        shift_acc = shift_acc + jnp.stack([shift_one, shift_two])
        grad_local = jnp.where(
            row_global[None, :, None], jnp.zeros((), jnp.bfloat16), grad_att
        ).reshape(per_micro, blocks_dev, BLOCK, H, HEAD)
        scores = local_scores(
            query_heads, shared_keys, random_keys, shared_ok, random_ok, scale_factor
        )
        local_probs = jnp.exp(scores - log_norm)
        local_weights = local_probs.astype(jnp.bfloat16)
        grad_prob = jnp.concatenate(
            [
                jnp.einsum(
                    "sbqhd,sbkhd->sbhqk",
                    grad_local,
                    shared_vals,
                    preferred_element_type=jnp.float32,
                ),
                jnp.einsum(
                    "sbqhd,sbhkd->sbhqk",
                    grad_local,
                    random_vals,
                    preferred_element_type=jnp.float32,
                ),
            ],
            axis=4,
        )
        row_delta = jnp.sum(local_probs * grad_prob, axis=4, keepdims=True)
        grad_score = (local_probs * (grad_prob - row_delta)).astype(jnp.bfloat16)
        grad_query = jnp.einsum(
            "sbhqk,sbkhd->sbqhd",
            grad_score[..., :shared_count],
            shared_keys,
            preferred_element_type=jnp.float32,
        )
        grad_query = (
            grad_query
            + jnp.einsum(
                "sbhqk,sbhkd->sbqhd",
                grad_score[..., shared_count:],
                random_keys,
                preferred_element_type=jnp.float32,
            )
        ) * scale_factor
        grad_key_shared = (
            jnp.einsum(
                "sbhqk,sbqhd->sbkhd",
                grad_score[..., :shared_count],
                query_heads,
                preferred_element_type=jnp.float32,
            )
            * scale_factor
        )
        grad_val_shared = jnp.einsum(
            "sbhqk,sbqhd->sbkhd",
            local_weights[..., :shared_count],
            grad_local,
            preferred_element_type=jnp.float32,
        )
        grad_key_random = (
            jnp.einsum(
                "sbhqk,sbqhd->sbhkd",
                grad_score[..., shared_count:],
                query_heads,
                preferred_element_type=jnp.float32,
            )
            * scale_factor
        )
        grad_val_random = jnp.einsum(
            "sbhqk,sbqhd->sbhkd",
            local_weights[..., shared_count:],
            grad_local,
            preferred_element_type=jnp.float32,
        )
        grad_shared = jnp.concatenate(
            [
                grad_key_shared.reshape(per_micro, blocks_dev, shared_count, features),
                grad_val_shared.reshape(per_micro, blocks_dev, shared_count, features),
            ],
            axis=3,
        )
        grad_window = grad_shared[:, :, : 3 * BLOCK].reshape(
            per_micro, blocks_dev, 3, BLOCK, 2 * features
        )
        ext_grad = jnp.zeros((per_micro, blocks_dev + 2, BLOCK, 2 * features), jnp.float32)
        for offset in range(3):
            ext_grad = ext_grad.at[:, offset : offset + blocks_dev].add(grad_window[:, :, offset])
        grad_glob_keys = jnp.sum(grad_shared[:, :, 3 * BLOCK :], axis=1)
        grad_random = jnp.stack([grad_key_random, grad_val_random], axis=4).reshape(
            per_micro, entries, BLOCK, 2 * HEAD
        )
        returned = (
            jnp.zeros((devices * capacity, per_micro, BLOCK, 2 * HEAD), jnp.float32)
            .at[positions, seq_ids[:, None]]
            .set(grad_random)
        )
        arrived = lax.all_to_all(
            returned.astype(jnp.bfloat16), "seq", split_axis=0, concat_axis=0, tiled=True
        ).astype(returned.dtype)
        arrived = arrived.reshape(devices, capacity, per_micro, BLOCK, 2 * HEAD) * live_mask[
            ..., None, None
        ].astype(jnp.float32)
        piece_grad = (
            jnp.zeros((per_micro, blocks_dev * H, BLOCK, 2 * HEAD), jnp.float32)
            .at[seq_ids[None, None, :], piece_index]
            .add(arrived)
        )
        piece_grad = (
            piece_grad.reshape(per_micro, blocks_dev, H, BLOCK, 2, HEAD)
            .transpose(0, 1, 3, 4, 2, 5)
            .reshape(per_micro, tok_dev, 2 * features)
        )
        rim_pair = jnp.concatenate([ext_grad[:, 0], ext_grad[:, blocks_dev + 1]], axis=1)
        rim_back = padded(rim_pair.astype(jnp.bfloat16), (("seq", 1),), BLOCK).astype(
            rim_pair.dtype
        )
        grad_kv = (
            ext_grad[:, 1 : blocks_dev + 1].reshape(per_micro, tok_dev, 2 * features) + piece_grad
        )
        grad_kv = grad_kv.at[:, :BLOCK].add(rim_back[:, :BLOCK])
        grad_kv = grad_kv.at[:, tok_dev - BLOCK :].add(rim_back[:, 3 * BLOCK :])
        grad_glob = from_root(grad_att[:, :glob_rows], "seq", 0)
        grad_glob_heads = grad_glob.reshape(per_micro, glob_rows, H, HEAD)
        glob_scores = (
            jnp.einsum(
                "sqhd,skhd->shqk", glob_query, local_keys, preferred_element_type=jnp.float32
            )
            * scale_factor
        )
        glob_probs = jnp.exp(glob_scores - glob_lse[..., None])
        glob_weights = glob_probs.astype(jnp.bfloat16)
        glob_grad_prob = jnp.einsum(
            "sqhd,skhd->shqk", grad_glob_heads, local_vals, preferred_element_type=jnp.float32
        )
        glob_delta = lax.psum(jnp.sum(glob_probs * glob_grad_prob, axis=3), "seq")
        glob_grad_score = (glob_probs * (glob_grad_prob - glob_delta[..., None])).astype(
            jnp.bfloat16
        )
        glob_grad_query = (
            jnp.einsum(
                "shqk,skhd->sqhd", glob_grad_score, local_keys, preferred_element_type=jnp.float32
            )
            * scale_factor
        )
        glob_grad_key = (
            jnp.einsum(
                "shqk,sqhd->skhd", glob_grad_score, glob_query, preferred_element_type=jnp.float32
            )
            * scale_factor
        )
        glob_grad_val = jnp.einsum(
            "shqk,sqhd->skhd", glob_weights, grad_glob_heads, preferred_element_type=jnp.float32
        )
        grad_kv = grad_kv + jnp.concatenate(
            [
                glob_grad_key.reshape(per_micro, tok_dev, features),
                glob_grad_val.reshape(per_micro, tok_dev, features),
            ],
            axis=2,
        )
        summed_query, summed_keys = lax.psum(
            (glob_grad_query.reshape(per_micro, glob_rows, features), grad_glob_keys), "seq"
        )
        grad_kv = grad_kv.at[:, :glob_rows].add(owner_flag * summed_keys)
        grad_queries = (
            grad_query.reshape(per_micro, tok_dev, features)
            .at[:, :glob_rows]
            .add(owner_flag * summed_query)
        )
        grad_qkv_rows = (
            jnp.concatenate([grad_queries, grad_kv], axis=2)
            .astype(jnp.bfloat16)
            .reshape(token_rows, 3 * features)
        )
        grad_qkv_w = grad_qkv_w + product_tn(tokens_flat, grad_qkv_rows)
        input_rows = grad_resid_one + product_nt(grad_qkv_rows, full_qkv)
        input_parts.append(input_rows.reshape(per_micro, tok_dev, features))
    summed = (
        lax.psum_scatter(grad_qkv_w, ("dp", "seq"), scatter_dimension=0, tiled=True),
        lax.psum_scatter(grad_out_w, ("dp", "seq"), scatter_dimension=0, tiled=True),
        lax.psum_scatter(grad_up_w, ("dp", "seq"), scatter_dimension=0, tiled=True),
        lax.psum_scatter(grad_down_w, ("dp", "seq"), scatter_dimension=0, tiled=True),
        lax.psum_scatter(gain_acc, ("dp", "seq"), scatter_dimension=1, tiled=True),
        lax.psum_scatter(shift_acc, ("dp", "seq"), scatter_dimension=1, tiled=True),
    )
    return (
        jnp.concatenate(output_parts, axis=0),
        jnp.concatenate(input_parts, axis=0),
        summed[0],
        summed[1],
        summed[2],
        summed[3],
        summed[4],
        summed[5],
    )


def solution(mesh):
    in_specs = (
        P("dp", "seq", None),
        P("dp", None),
        P("dp", None, None, None),
        P("dp", None),
        P("dp", None),
        P("dp", None),
        P("dp", None),
        P(),
        P(),
        P("dp", "seq", None),
    )
    out_specs = (
        P("dp", "seq", None),
        P("dp", "seq", None),
        P(("dp", "seq"), None),
        P(("dp", "seq"), None),
        P(("dp", "seq"), None),
        P(("dp", "seq"), None),
        P(None, ("dp", "seq")),
        P(None, ("dp", "seq")),
    )
    return jax.shard_map(
        per_device, mesh=mesh, in_specs=in_specs, out_specs=out_specs, check_vma=False
    )
```

profile of v0, /device:TPU:0, one launch (start us, length us, event | category | flops | bytes accessed | tf_op | source)
XLA Modules:
  0.0 1229.0 jit_solution(650934063268658382)
XLA Ops:
  8.0 51.7 %all-gather.13.cloned.1.call-done = bf16[768,2304]{1,0:T(8,128)(2,1)} async-done(((bf16[192,2304]{1,0:T(8,128)(2,1)}), bf16[768,2304]{1,0:T(8,128)(2,1)}) %all-gather.13.cloned.1.call-update) | async-done | bytes 3538960 | tf_op jit(solution)/shard_map/all_gather | solution.py:164
  106.0 4.7 all-to-all-start.1
  126.7 4.2 collective-permute-start
  157.7 35.9 %all-gather.5 = f32[8,12,128]{2,1,0:T(8,128)S(1)} all-gather(f32[1,12,128]{2,1,0:T(8,128)S(1)} %bitcast.675), channel_id=3, replica_groups=mesh['dp'=4,'seq'=8] {'seq'}, dimensions={0}, use_global_device_ids=true | all-gather | bytes 55296 | tf_op jit(solution)/shard_map/all_gather | solution.py:43
  194.2 14.5 %all-gather.4 = f32[8,12,128]{2,1,0:T(8,128)S(1)} all-gather(f32[1,12,128]{2,1,0:T(8,128)S(1)} %bitcast.673), channel_id=2, replica_groups=mesh['dp'=4,'seq'=8] {'seq'}, dimensions={0}, use_global_device_ids=true | all-gather | bytes 55296 | tf_op jit(solution)/shard_map/all_gather | solution.py:43
  209.3 9.5 while.49
  227.6 14.0 %all-gather.7 = f32[8,12,128]{2,1,0:T(8,128)S(1)} all-gather(f32[1,12,128]{2,1,0:T(8,128)S(1)} %bitcast.676), channel_id=5, replica_groups=mesh['dp'=4,'seq'=8] {'seq'}, dimensions={0}, use_global_device_ids=true | all-gather | bytes 55296 | tf_op jit(solution)/shard_map/all_gather | solution.py:43
  242.2 14.0 %all-gather.6 = f32[8,12,128]{2,1,0:T(8,128)S(1)} all-gather(f32[1,12,128]{2,1,0:T(8,128)S(1)} %bitcast.674), channel_id=4, replica_groups=mesh['dp'=4,'seq'=8] {'seq'}, dimensions={0}, use_global_device_ids=true | all-gather | bytes 55296 | tf_op jit(solution)/shard_map/all_gather | solution.py:43
  256.8 9.5 while.50
  285.2 35.0 %all-reduce.30 = (bf16[1,128,768]{2,1,0:T(8,128)(2,1)}, bf16[1,128,768]{2,1,0:T(8,128)(2,1)}) all-reduce(f32[1,128,768]{2,1,0:T(8,128)} %copy.430, f32[1,128,768]{2,1,0:T(8,128)} %copy.406), channel_id=1, replica_groups=mesh['dp'=4,'seq'=8] {'seq'}, use_global_device_ids=true, to_apply=%region_20.22 | all-reduce | flops 196608 | bytes 1179648 | tf_op jit(solution)/shard_map/psum | solution.py:279
  320.2 4.3 all-to-all-start
  328.4 7.2 reshape.2648
  335.6 19.9 %fusion.177 = (bf16[1,3,12,3,64,1,64]{6,5,4,3,2,1,0:T(2,128)(2,1)}, bf16[1,3,12,3,64,1,64]{6,5,4,3,2,1,0:T(2,128)(2,1)}) fusion(bf16[1,3,12,3,64,2,64]{6,5,4,3,2,1,0:T(2,128)(2,1)} %reshape.2648), kind=kLoop, calls=%fused_computation.467 | loop fusion | bytes 3538944 | tf_op jit(solution)/shard_map/slice | solution.py:207
  381.5 7.2 reshape.2625
  388.7 19.9 %fusion.176 = (bf16[1,3,12,3,64,1,64]{6,5,4,3,2,1,0:T(2,128)(2,1)}, bf16[1,3,12,3,64,1,64]{6,5,4,3,2,1,0:T(2,128)(2,1)}) fusion(bf16[1,3,12,3,64,2,64]{6,5,4,3,2,1,0:T(2,128)(2,1)} %reshape.2625), kind=kLoop, calls=%fused_computation.466 | loop fusion | bytes 3538944 | tf_op jit(solution)/shard_map/slice | solution.py:207
  437.5 5.1 fusion.164
  442.6 4.6 fusion.188
  475.3 4.5 convolution_bitcast_fusion.7
  488.4 4.3 convolution_bitcast_fusion
  492.7 4.6 convolution_bitcast_fusion.6
  497.3 5.6 multiply_reduce_fusion.1
  502.9 5.9 multiply_convert_fusion.1
  514.6 4.2 convolution_multiply_fusion.3
  518.7 4.1 fusion.31
  522.9 4.2 multiply_reduce_fusion
  527.1 5.1 multiply_convert_fusion
  541.8 5.9 copy.460
  547.6 4.9 copy.481
  552.5 5.0 copy.480
  562.0 30.6 %all-reduce.27.cloned.1.call-done = (bf16[128,12,64]{0,2,1:T(8,128)(2,1)}, bf16[128,12,64]{0,2,1:T(8,128)(2,1)}) async-done(((bf16[128,12,64]{0,2,1:T(8,128)(2,1)}, bf16[128,12,64]{0,2,1:T(8,128)(2,1)}), (bf16[128,12,64]{0,2,1:T(8,128)(2,1)}, bf16[128,12,64]{0,2,1:T(8,128)(2,1)})) %all-reduce.27.cloned.1.call-update) | async-done | bytes 393232 | tf_op jit(solution)/shard_map/psum | solution.py:39
  597.0 26.5 %all-reduce.15 = (f32[12,128]{1,0:T(8,128)}, f32[12,128]{1,0:T(8,128)}) all-reduce(f32[12,128]{1,0:T(8,128)S(1)} %get-tuple-element.690, f32[12,128]{1,0:T(8,128)S(1)} %copy-done.173), channel_id=1, replica_groups=mesh['dp'=4,'seq'=8] {'seq'}, use_global_device_ids=true, to_apply=%region_50.52 | all-reduce | flops 3072 | bytes 24576 | tf_op jit(solution)/shard_map/psum | solution.py:446
  641.6 5.1 convolution_add_fusion
  688.1 10.1 copy.465
  698.2 7.9 reshape.2901
  708.4 17.3 %scatter_fusion = f32[112,64,128]{2,1,0:T(8,128)} fusion(f32[112,64,128]{2,1,0:T(8,128)} %broadcast.1738.clone.1, s32[108]{0:T(128)S(1)} %copy-done.205, f32[108,64,128]{2,1,0:T(8,128)} %reshape.2901), kind=kCustom, calls=%fused_computation.10 | custom fusion | bytes 10617264 | tf_op jit(solution)/shard_map/scatter | solution.py:406
  729.5 4.3 all-to-all-start.2
  742.6 4.2 fusion.14
  748.5 5.1 convolution_add_fusion.1
  764.9 10.1 copy.487
  775.0 7.9 reshape.2925
  794.0 17.0 %scatter_fusion.2 = f32[112,64,128]{2,1,0:T(8,128)} fusion(f32[112,64,128]{2,1,0:T(8,128)} %broadcast.1738.clone, s32[108]{0:T(128)S(1)} %copy-done.204, f32[108,64,128]{2,1,0:T(8,128)} %reshape.2925), kind=kCustom, calls=%fused_computation.12 | custom fusion | bytes 10617264 | tf_op jit(solution)/shard_map/scatter | solution.py:406
  817.5 4.6 all-to-all-start.3
  837.5 12.4 %scatter_fusion.1 = f32[36,64,128]{2,1,0:T(8,128)S(1)} fusion(f32[36,64,128]{2,1,0:T(8,128)S(1)} %broadcast.1736.clone.1, s32[112]{0:T(128)S(1)} %copy-done.162, f32[112,64,128]{2,1,0:T(8,128)} %bitcast.620), kind=kCustom, calls=%fused_computation.11 | custom fusion | flops 917504 | bytes 11010496 | tf_op jit(solution)/shard_map/scatter-add | solution.py:417
  869.8 12.0 scatter_fusion.3
  901.2 8.2 copy.502
  914.1 40.5 %all-reduce.14 = (f32[2,768]{1,0:T(2,128)}, f32[2,768]{1,0:T(2,128)}) all-reduce(f32[2,768]{1,0:T(2,128)S(1)} %maximum_add_fusion.2, f32[2,768]{1,0:T(2,128)S(1)} %maximum_add_fusion.3), channel_id=10, replica_groups=mesh['dp'=4,'seq'=8] {'dp','seq'}, use_global_device_ids=true, to_apply=%region_64.66.clone | all-reduce | flops 3072 | bytes 24576
  964.4 133.2 %reduce-scatter.11.cloned.1.call-done = f32[24,3072]{1,0:T(8,128)} async-done(((f32[768,3072]{1,0:T(8,128)}), f32[24,3072]{1,0:T(8,128)}) %reduce-scatter.11.cloned.1.call-update) | async-done | bytes 294928 | tf_op jit(solution)/shard_map/reduce_scatter | solution.py:492
  1097.6 124.8 %reduce-scatter.15.cloned.1.call-done = f32[24,2304]{1,0:T(8,128)} async-done(((f32[768,2304]{1,0:T(8,128)}), f32[24,2304]{1,0:T(8,128)}) %reduce-scatter.15.cloned.1.call-update) | async-done | bytes 221200
  (823 shorter events, 429.8 us)
Async XLA Ops:
  7.2 52.5 %all-gather.13.cloned.1.call-start = ((), (), s32[]{:S(2)}) async-start(), calls=%async_computation.8 | async-start | bytes 4423680 | tf_op jit(solution)/shard_map/all_gather | solution.py:164
  7.9 142.7 %all-reduce.29.cloned.1.call-start = ((), (), s32[]{:S(2)}) async-start(), calls=%async_computation.18 | async-start | bytes 2359296 | tf_op jit(solution)/shard_map/psum | solution.py:39
  8.0 54.9 %copy-start.90 = (bf16[2,192,768]{2,1,0:T(8,128)(2,1)S(1)}, bf16[2,192,768]{2,1,0:T(8,128)(2,1)}, u32[]{:S(2)}) copy-start(bf16[2,192,768]{2,1,0:T(8,128)(2,1)} %param.47) | copy-start | bytes 1769476
  64.9 369.6 %all-gather.15.cloned.1.call-start = ((), (), s32[]{:S(2)}) async-start(), calls=%async_computation.9 | async-start | bytes 1474560 | tf_op jit(solution)/shard_map/all_gather | solution.py:165
  65.6 371.9 %all-gather.17.cloned.1.call-start = ((), (), s32[]{:S(2)}) async-start(), calls=%async_computation.10 | async-start | bytes 5898240 | tf_op jit(solution)/shard_map/all_gather | solution.py:166
  66.2 376.4 %all-gather.19.cloned.1.call-start = ((), (), s32[]{:S(2)}) async-start(), calls=%async_computation.11 | async-start | bytes 5898240 | tf_op jit(solution)/shard_map/all_gather | solution.py:167
  67.4 14.9 %copy-start.206 = (s32[9]{0:T(128)S(1)}, s32[9]{0:T(128)}, u32[]{:S(2)}) copy-start(s32[9]{0:T(128)} %constant.690) | copy-start | bytes 112
  69.6 18.3 %copy-start.192 = (f32[2,768]{1,0:T(2,128)S(1)}, f32[2,768]{1,0:T(2,128)}, u32[]{:S(2)}) copy-start(f32[2,768]{1,0:T(2,128)} %param.54) | copy-start | bytes 18436
  69.6 18.9 %copy-start.193 = (f32[2,768]{1,0:T(2,128)S(1)}, f32[2,768]{1,0:T(2,128)}, u32[]{:S(2)}) copy-start(f32[2,768]{1,0:T(2,128)} %param.55) | copy-start | bytes 18436
  82.3 56.2 %copy-start.184 = (s32[1024]{0:T(1024)}, s32[1024]{0:T(1024)S(1)}, u32[]{:S(2)}) copy-start(s32[1024]{0:T(1024)S(1)} %pad_clamp_fusion.1) | copy-start | bytes 12292
  92.6 28.1 %copy-start.86 = (bf16[1,192,1536]{2,1,0:T(8,128)(2,1)}, bf16[1,192,1536]{2,1,0:T(8,128)(2,1)S(1)}, u32[]{:S(2)}) copy-start(bf16[1,192,1536]{2,1,0:T(8,128)(2,1)S(1)} %slice.754) | copy-start | bytes 1769476
  106.0 214.2 %all-to-all-start.1 = ((bf16[112,1,64,128]{3,2,1,0:T(8,128)(2,1)}), bf16[112,1,64,128]{3,2,1,0:T(8,128)(2,1)}, u32[]{:S(2)}, u32[]{:S(2)}) async-start(bf16[112,1,64,128]{3,2,1,0:T(8,128)(2,1)} %fusion.26), calls=%async_computation.1 | async-start | bytes 3670016 | tf_op jit(solution)/shard_map/all_to_all | solution.py:199
  112.6 24.8 %collective-permute-start.2 = (bf16[1,64,1536]{2,1,0:T(8,128)(2,1)}, bf16[1,64,1536]{2,1,0:T(8,128)(2,1)}, u32[]{:S(2)}, u32[]{:S(2)}) collective-permute-start(bf16[1,64,1536]{2,1,0:T(8,128)(2,1)} %get-tuple-element.646), channel_id=1, source_target_pairs={{0,1},{1,2},{2,3},{3,4},{4,5},{5,6},{6,7},{8,9},{9,10},{10,11},{11... | collective-permute-start | bytes 589832 | tf_op jit(solution)/shard_map/ppermute | solution.py:28
  115.7 21.7 %collective-permute-start.3 = (bf16[1,64,1536]{2,1,0:T(8,128)(2,1)}, bf16[1,64,1536]{2,1,0:T(8,128)(2,1)}, u32[]{:S(2)}, u32[]{:S(2)}) collective-permute-start(bf16[1,64,1536]{2,1,0:T(8,128)(2,1)} %get-tuple-element.647), channel_id=1, source_target_pairs={{1,0},{2,1},{3,2},{4,3},{5,4},{6,5},{7,6},{9,8},{10,9},{11,10},{12... | collective-permute-start | bytes 589832 | tf_op jit(solution)/shard_map/ppermute | solution.py:30
  126.7 16.5 %collective-permute-start = (bf16[1,64,1536]{2,1,0:T(8,128)(2,1)}, bf16[1,64,1536]{2,1,0:T(8,128)(2,1)}, u32[]{:S(2)}, u32[]{:S(2)}) collective-permute-start(bf16[1,64,1536]{2,1,0:T(8,128)(2,1)} %get-tuple-element.638), channel_id=1, source_target_pairs={{0,1},{1,2},{2,3},{3,4},{4,5},{5,6},{6,7},{8,9},{9,10},{10,11},{11... | collective-permute-start | bytes 589832 | tf_op jit(solution)/shard_map/ppermute | solution.py:28
  130.9 12.3 %collective-permute-start.1 = (bf16[1,64,1536]{2,1,0:T(8,128)(2,1)}, bf16[1,64,1536]{2,1,0:T(8,128)(2,1)}, u32[]{:S(2)}, u32[]{:S(2)}) collective-permute-start(bf16[1,64,1536]{2,1,0:T(8,128)(2,1)} %get-tuple-element.639), channel_id=1, source_target_pairs={{1,0},{2,1},{3,2},{4,3},{5,4},{6,5},{7,6},{9,8},{10,9},{11,10},{12... | collective-permute-start | bytes 589832 | tf_op jit(solution)/shard_map/ppermute | solution.py:30
  157.5 68.4 %copy-start.6 = (f32[12,128,192]{1,2,0:T(8,128)}, f32[12,128,192]{1,2,0:T(8,128)S(1)}, u32[]{:S(2)}) copy-start(f32[12,128,192]{1,2,0:T(8,128)S(1)} %get-tuple-element.678) | copy-start | bytes 3538948
  193.5 15.7 %copy-start.155 = (f32[8,12,128]{2,1,0:T(8,128)}, f32[8,12,128]{2,1,0:T(8,128)S(1)}, u32[]{:S(2)}) copy-start(f32[8,12,128]{2,1,0:T(8,128)S(1)} %all-gather.5) | copy-start | bytes 147460
  227.4 46.0 %copy-start.8 = (f32[12,128,192]{1,2,0:T(8,128)}, f32[12,128,192]{1,2,0:T(8,128)S(1)}, u32[]{:S(2)}) copy-start(f32[12,128,192]{1,2,0:T(8,128)S(1)} %get-tuple-element.676) | copy-start | bytes 3538948
  241.6 15.2 %copy-start.153 = (f32[8,12,128]{2,1,0:T(8,128)}, f32[8,12,128]{2,1,0:T(8,128)S(1)}, u32[]{:S(2)}) copy-start(f32[8,12,128]{2,1,0:T(8,128)S(1)} %all-gather.7) | copy-start | bytes 147460
  320.2 57.6 %all-to-all-start = ((bf16[112,1,64,128]{3,2,1,0:T(8,128)(2,1)}), bf16[112,1,64,128]{3,2,1,0:T(8,128)(2,1)}, u32[]{:S(2)}, u32[]{:S(2)}) async-start(bf16[112,1,64,128]{3,2,1,0:T(8,128)(2,1)} %fusion.27), calls=%async_computation | async-start | bytes 3670016 | tf_op jit(solution)/shard_map/all_to_all | solution.py:199
  324.5 268.0 %all-reduce.27.cloned.1.call-start = ((), (), s32[]{:S(2)}) async-start(), calls=%async_computation.17 | async-start | bytes 786432 | tf_op jit(solution)/shard_map/psum | solution.py:39
  436.4 31.8 %copy-start.159 = (f32[192]{0:T(256)}, f32[192]{0:T(256)S(1)}, u32[]{:S(2)}) copy-start(f32[192]{0:T(256)S(1)} %broadcast_multiply_fusion.9) | copy-start | bytes 2308
  447.2 18.2 %copy-start.76 = (f32[192,768]{1,0:T(8,128)}, f32[192,768]{1,0:T(8,128)S(1)}, u32[]{:S(2)}) copy-start(f32[192,768]{1,0:T(8,128)S(1)} %get-tuple-element.686) | copy-start | bytes 1769476
  447.2 18.2 %copy-start.176 = (f32[192]{0:T(256)}, f32[192]{0:T(256)S(1)}, u32[]{:S(2)}) copy-start(f32[192]{0:T(256)S(1)} %broadcast_multiply_fusion.8) | copy-start | bytes 2308
  447.5 18.0 %copy-start.189 = (f32[192]{0:T(256)}, f32[192]{0:T(256)S(1)}, u32[]{:S(2)}) copy-start(f32[192]{0:T(256)S(1)} %add_rsqrt_fusion) | copy-start | bytes 2308
  448.0 17.4 %copy-start.64 = (f32[192,768]{1,0:T(8,128)}, f32[192,768]{1,0:T(8,128)S(1)}, u32[]{:S(2)}) copy-start(f32[192,768]{1,0:T(8,128)S(1)} %get-tuple-element.680) | copy-start | bytes 1769476
  448.0 17.4 %copy-start.166 = (f32[192]{0:T(256)}, f32[192]{0:T(256)S(1)}, u32[]{:S(2)}) copy-start(f32[192]{0:T(256)S(1)} %broadcast_multiply_fusion.11) | copy-start | bytes 2308
  448.3 17.2 %copy-start.174 = (f32[192]{0:T(256)}, f32[192]{0:T(256)S(1)}, u32[]{:S(2)}) copy-start(f32[192]{0:T(256)S(1)} %add_rsqrt_fusion.3) | copy-start | bytes 2308
  535.2 295.5 %all-reduce.25.cloned.1.call-start = ((), (), s32[]{:S(2)}) async-start(), calls=%async_computation.16 | async-start | bytes 4718592 | tf_op jit(solution)/shard_map/psum | solution.py:472
  541.8 15.8 %copy-start.23 = (f32[1,3,320,768]{3,2,1,0:T(8,128)}, f32[1,3,320,768]{3,2,1,0:T(8,128)S(1)}, u32[]{:S(2)}) copy-start(f32[1,3,320,768]{3,2,1,0:T(8,128)S(1)} %copy.459) | copy-start | bytes 8847364
  560.9 31.6 %copy-start.7 = (f32[12,128,192]{1,2,0:T(8,128)S(1)}, f32[12,128,192]{1,2,0:T(8,128)}, u32[]{:S(2)}) copy-start(f32[12,128,192]{1,2,0:T(8,128)} %copy-done.6) | copy-start | bytes 3538948
  560.9 31.6 %copy-start.96 = (bf16[1,192,768]{1,2,0:T(8,128)(2,1)S(1)}, bf16[1,192,768]{1,2,0:T(8,128)(2,1)}, u32[]{:S(2)}) copy-start(bf16[1,192,768]{1,2,0:T(8,128)(2,1)} %copy.401) | copy-start | bytes 884740
  560.9 31.7 %copy-start.149 = (f32[12,128]{1,0:T(8,128)S(1)}, f32[12,128]{1,0:T(8,128)}, u32[]{:S(2)}) copy-start(f32[12,128]{1,0:T(8,128)} %copy-done.148) | copy-start | bytes 18436
  562.0 33.6 %copy-start.9 = (f32[12,128,192]{1,2,0:T(8,128)S(1)}, f32[12,128,192]{1,2,0:T(8,128)}, u32[]{:S(2)}) copy-start(f32[12,128,192]{1,2,0:T(8,128)} %copy-done.8) | copy-start | bytes 3538948
  633.9 330.5 %reduce-scatter.9.cloned.1.call-start = ((), (), s32[]{:S(2)}) async-start(), calls=%async_computation.12 | async-start | bytes 2433024 | tf_op jit(solution)/shard_map/reduce_scatter | solution.py:491
  637.6 326.7 %reduce-scatter.13.cloned.1.call-start = ((), (), s32[]{:S(2)}) async-start(), calls=%async_computation.14 | async-start | bytes 9732096 | tf_op jit(solution)/shard_map/reduce_scatter | solution.py:493
  729.5 88.1 %all-to-all-start.2 = ((bf16[112,1,64,128]{3,2,1,0:T(8,128)(2,1)}), bf16[112,1,64,128]{3,2,1,0:T(8,128)(2,1)}, u32[]{:S(2)}, u32[]{:S(2)}) async-start(bf16[112,1,64,128]{3,2,1,0:T(8,128)(2,1)} %convert_bitcast_fusion.1), calls=%async_computation.2 | async-start | bytes 3670016 | tf_op jit(solution)/shard_map/all_to_all | solution.py:408
  733.8 363.7 %reduce-scatter.11.cloned.1.call-start = ((), (), s32[]{:S(2)}) async-start(), calls=%async_computation.13 | async-start | bytes 9732096 | tf_op jit(solution)/shard_map/reduce_scatter | solution.py:492
  735.6 123.9 %collective-permute-start.5 = (bf16[1,64,1536]{2,1,0:T(8,128)(2,1)}, bf16[1,64,1536]{2,1,0:T(8,128)(2,1)}, u32[]{:S(2)}, u32[]{:S(2)}) collective-permute-start(bf16[1,64,1536]{2,1,0:T(8,128)(2,1)} %get-tuple-element.631), channel_id=1, source_target_pairs={{1,0},{2,1},{3,2},{4,3},{5,4},{6,5},{7,6},{9,8},{10,9},{11,10},{12... | collective-permute-start | bytes 589832 | tf_op jit(solution)/shard_map/ppermute | solution.py:30
  738.7 120.8 %collective-permute-start.4 = (bf16[1,64,1536]{2,1,0:T(8,128)(2,1)}, bf16[1,64,1536]{2,1,0:T(8,128)(2,1)}, u32[]{:S(2)}, u32[]{:S(2)}) collective-permute-start(bf16[1,64,1536]{2,1,0:T(8,128)(2,1)} %get-tuple-element.634), channel_id=1, source_target_pairs={{0,1},{1,2},{2,3},{3,4},{4,5},{5,6},{6,7},{8,9},{9,10},{10,11},{11... | collective-permute-start | bytes 589832 | tf_op jit(solution)/shard_map/ppermute | solution.py:28
  784.6 107.6 %collective-permute-start.7 = (bf16[1,64,1536]{2,1,0:T(8,128)(2,1)}, bf16[1,64,1536]{2,1,0:T(8,128)(2,1)}, u32[]{:S(2)}, u32[]{:S(2)}) collective-permute-start(bf16[1,64,1536]{2,1,0:T(8,128)(2,1)} %get-tuple-element.633), channel_id=1, source_target_pairs={{1,0},{2,1},{3,2},{4,3},{5,4},{6,5},{7,6},{9,8},{10,9},{11,10},{12... | collective-permute-start | bytes 589832 | tf_op jit(solution)/shard_map/ppermute | solution.py:30
  787.6 104.6 %collective-permute-start.6 = (bf16[1,64,1536]{2,1,0:T(8,128)(2,1)}, bf16[1,64,1536]{2,1,0:T(8,128)(2,1)}, u32[]{:S(2)}, u32[]{:S(2)}) collective-permute-start(bf16[1,64,1536]{2,1,0:T(8,128)(2,1)} %get-tuple-element.636), channel_id=1, source_target_pairs={{0,1},{1,2},{2,3},{3,4},{4,5},{5,6},{6,7},{8,9},{9,10},{10,11},{11... | collective-permute-start | bytes 589832 | tf_op jit(solution)/shard_map/ppermute | solution.py:28
  794.0 17.0 %copy-start.134 = (bf16[64,1536]{1,0:T(8,128)(2,1)S(1)}, bf16[64,1536]{1,0:T(8,128)(2,1)}, u32[]{:S(2)}) copy-start(bf16[64,1536]{1,0:T(8,128)(2,1)} %get-tuple-element.630) | copy-start | bytes 589828
  794.0 17.0 %copy-start.135 = (bf16[64,1536]{1,0:T(8,128)(2,1)S(1)}, bf16[64,1536]{1,0:T(8,128)(2,1)}, u32[]{:S(2)}) copy-start(bf16[64,1536]{1,0:T(8,128)(2,1)} %get-tuple-element.635) | copy-start | bytes 589828
  817.5 48.5 %all-to-all-start.3 = ((bf16[112,1,64,128]{3,2,1,0:T(8,128)(2,1)}), bf16[112,1,64,128]{3,2,1,0:T(8,128)(2,1)}, u32[]{:S(2)}, u32[]{:S(2)}) async-start(bf16[112,1,64,128]{3,2,1,0:T(8,128)(2,1)} %convert_bitcast_fusion), calls=%async_computation.3 | async-start | bytes 3670016 | tf_op jit(solution)/shard_map/all_to_all | solution.py:408
  822.2 400.1 %reduce-scatter.15.cloned.1.call-start = ((), (), s32[]{:S(2)}) async-start(), calls=%async_computation.15 | async-start | bytes 7299072
  909.4 49.7 %copy-start.63 = (bf16[768,2304]{1,0:T(8,128)(2,1)S(1)}, bf16[768,2304]{1,0:T(8,128)(2,1)}, u32[]{:S(2)}) copy-start(bf16[768,2304]{1,0:T(8,128)(2,1)} %all-gather.13.cloned.1.call-done) | copy-start | bytes 10616836
  (186 other events, 672.7 us)
Sparse Core Ops, SparseCore 0:
  9.8 49.8 all-gather.12
  65.0 66.5 all-reduce.28
  133.5 32.2 all-gather.14
  167.5 56.9 all-gather.16
  226.1 56.9 all-gather.18
  535.3 57.1 all-reduce.26
  634.0 65.2 all-reduce.24
  705.2 108.1 reduce-scatter.8
  819.8 136.1 reduce-scatter.12
  962.4 135.1 reduce-scatter.10
  1103.8 118.4 reduce-scatter.14
where the time goes:
time: 1240 us; the launch traced here: 1230 us
  waiting for transfers between devices  345 us (28%)
  local copies, waits for them, and re-layouts  340 us (27%)
  blocking collectives  180 us (15%)
  other arithmetic  173 us (14%)
  matrix products  135 us (11%)
  starting transfers between devices  39 us (3%)
  between operations  17 us (1%)
    reduce_scatter x1, waiting for transfers between devices, per_device(): lax.psum_scatter(grad_up_w, ('dp', 'seq'), scatter_dimension=0, tiled=True)  133 us
    unnamed x12, waiting for transfers between devices  127 us
    all_gather x4, blocking collectives, merged(): everything = jax.tree.map(lambda part: lax.all_gather(part, axis), x)  78.3 us
    all_gather x1, waiting for transfers between devices, per_device(): lax.all_gather(w_qkv, 'dp', axis=0, tiled=True)  51.7 us
    unnamed x1, blocking collectives  40.5 us
    slice x2, local copies, waits for them, and re-layouts, per_device(): fetched[..., 0, :].reshape(per_micro, blocks_dev, H, R * BLOCK, HEAD)  39.8 us
    unnamed x431, local copies, waits for them, and re-layouts  37.6 us
    psum x1, blocking collectives, per_device(): glob_out = lax.psum(glob_part, 'seq')  35 us
  transfers between devices with their start and end apart: 23, of which 5 were waited for; matrix products, arithmetic and copies ran while one was open for 42% of the time, Pallas kernels for 0%

commit v1 on v0

--- a/solution.py
+++ b/solution.py
@@ -2,6 +2,8 @@
 import jax.numpy as jnp
 import numpy as np
 from jax import lax
+from jax.experimental import pallas as pl
+from jax.experimental.pallas import tpu as pltpu
 from jax.sharding import PartitionSpec as P
 
 H = 12
@@ -506,6 +508,803 @@
     )
 
 
+TILE = 128
+NH = 3
+CH = 256
+LOG2E = 1.4426950408889634
+SCALE2 = HEAD ** (-0.5) * LOG2E
+NEG = -1e30
+F32 = jnp.float32
+BF16 = jnp.bfloat16
+
+
+def nt(a, b):
+    return lax.dot_general(a, b, (((1,), (1,)), ((), ())), preferred_element_type=F32)
+
+
+def nn(a, b):
+    return jnp.dot(a, b, preferred_element_type=F32)
+
+
+def biased(s, mask, b1_ref, b0_ref, first_block):
+    rows = []
+    for j in range(s.shape[0] // BLOCK):
+        kb = first_block + j
+        m3 = jnp.concatenate([mask[BLOCK * j : BLOCK * (j + 1)]] * NH, axis=1)
+        on = b1_ref[0, kb : kb + 1, :]
+        off = jnp.concatenate([b0_ref[0, kb : kb + 1, :]] * NH, axis=1)
+        rows.append(s[BLOCK * j : BLOCK * (j + 1)] * SCALE2 + jnp.where(m3, on, off))
+    return jnp.concatenate(rows, axis=0)
+
+
+def forward_kernel(
+    xs, wg, b1, b0, segk, segq, att, otile, lse, qn, kn, vn, qt, kt, vt, q3, tbuf
+):
+    step = pl.program_id(0)
+    length = xs.shape[0]
+    chunks = length // CH
+
+    @pl.when(step == 0)
+    def _():
+        q3[...] = jnp.zeros_like(q3)
+        for j in range(chunks):
+            rows = slice(CH * j, CH * (j + 1))
+            both = nn(xs[rows, :], wg[...])
+            qf, kf, vf = both[:, :256], both[:, 256:512], both[:, 512:]
+            qn[rows, :] = qf.astype(BF16)
+            kn[rows, :] = kf.astype(BF16)
+            vn[rows, :] = vf.astype(BF16)
+            qt[:, rows] = qf.T.astype(BF16)
+            kt[:, rows] = kf.T.astype(BF16)
+            vt[:, rows] = vf.T.astype(BF16)
+
+    cols = pl.ds(pl.multiple_of(step * TILE, TILE), TILE)
+    for h in range(NH):
+        q3[HEAD * h : HEAD * (h + 1), TILE * h : TILE * (h + 1)] = qt[
+            HEAD * h : HEAD * (h + 1), cols
+        ]
+    top = jnp.full((8, NH * TILE), NEG, F32)
+    for j in range(chunks):
+        rows = slice(CH * j, CH * (j + 1))
+        s = nn(kn[rows, :], q3[...])
+        t = biased(s, segk[rows, :] == segq[0], b1, b0, CH // BLOCK * j)
+        tbuf[rows, :] = t
+        top = jnp.maximum(top, jnp.max(t.reshape(CH // 8, 8, NH * TILE), axis=0))
+    peak = jnp.max(top, axis=0, keepdims=True)
+    total = jnp.zeros((8, NH * TILE), F32)
+    out = jnp.zeros((256, NH * TILE), F32)
+    for j in range(chunks):
+        rows = slice(CH * j, CH * (j + 1))
+        p = jnp.exp2(tbuf[rows, :] - peak)
+        total = total + jnp.sum(p.reshape(CH // 8, 8, NH * TILE), axis=0)
+        out = out + nn(vt[:, rows], p.astype(BF16))
+    weight = jnp.sum(total, axis=0, keepdims=True)
+    lse[0] = peak + jnp.log2(weight)
+    inv = 1.0 / weight
+    heads = [
+        out[HEAD * h : HEAD * (h + 1), TILE * h : TILE * (h + 1)] * inv[:, TILE * h : TILE * (h + 1)]
+        for h in range(NH)
+    ]
+    merged = jnp.concatenate(heads, axis=0)
+    otile[0] = merged
+    att[...] = merged.T.astype(BF16)
+
+
+def attend_forward(xs, wg, b1, b0, segk, segq):
+    length = xs.shape[0]
+    steps = length // TILE
+    blocks = length // BLOCK
+    whole = lambda *shape: pl.BlockSpec(shape, lambda i: (0,) * len(shape))
+    per = lambda *shape: pl.BlockSpec((1,) + shape, lambda i: (i,) + (0,) * len(shape))
+    nat = jax.ShapeDtypeStruct((length, 256), BF16)
+    tra = jax.ShapeDtypeStruct((256, length), BF16)
+    return pl.pallas_call(
+        forward_kernel,
+        grid=(steps,),
+        in_specs=[
+            whole(*xs.shape), whole(*wg.shape), per(blocks, NH * TILE), per(blocks, TILE),
+            whole(*segk.shape), per(1, TILE),
+        ],
+        out_specs=[
+            pl.BlockSpec((TILE, NH * HEAD), lambda i: (i, 0)), per(NH * HEAD, TILE), per(1, NH * TILE),
+            whole(length, 256), whole(length, 256), whole(length, 256),
+            whole(256, length), whole(256, length),
+        ],
+        out_shape=[
+            jax.ShapeDtypeStruct((length, NH * HEAD), BF16),
+            jax.ShapeDtypeStruct((steps, NH * HEAD, TILE), F32),
+            jax.ShapeDtypeStruct((steps, 1, NH * TILE), F32),
+            nat, nat, nat, tra, tra,
+        ],
+        scratch_shapes=[
+            pltpu.VMEM((256, length), BF16),
+            pltpu.VMEM((256, NH * TILE), BF16),
+            pltpu.VMEM((length, NH * TILE), F32),
+        ],
+        name="attend_forward",
+    )(xs, wg, b1, b0, segk, segq)
+
+
+def backward_kernel(
+    dat, qn, qt, otile, lse, b1, b0, segk, segq, kn, vn, kt, dqkv, q3t, d3t, q3, d3, dk, dv
+):
+    step = pl.program_id(0)
+    steps = pl.num_programs(0)
+    length = kn.shape[0]
+    chunks = length // CH
+
+    @pl.when(step == 0)
+    def _():
+        q3t[...] = jnp.zeros_like(q3t)
+        d3t[...] = jnp.zeros_like(d3t)
+        dk[...] = jnp.zeros_like(dk)
+        dv[...] = jnp.zeros_like(dv)
+
+    dat_f = dat[...].astype(F32)
+    dat_t = dat_f.T
+    lane = lax.broadcasted_iota(jnp.int32, (TILE, NH * HEAD), 1) // HEAD
+    qblk = qn[:, : NH * HEAD].astype(F32)
+    delta = []
+    for h in range(NH):
+        hr = slice(HEAD * h, HEAD * (h + 1))
+        hc = slice(TILE * h, TILE * (h + 1))
+        q3t[hr, hc] = qt[hr, :]
+        d3t[hr, hc] = dat_t[hr].astype(BF16)
+        q3[hc, :] = jnp.where(lane == h, qblk, 0.0).astype(BF16)
+        d3[hc, :] = jnp.where(lane == h, dat_f, 0.0).astype(BF16)
+        delta.append(jnp.sum(dat_t[hr] * otile[0, hr, :], axis=0, keepdims=True))
+    delta = jnp.concatenate(delta, axis=1)
+    norm = lse[0]
+    dq = jnp.zeros((256, NH * TILE), F32)
+    for j in range(chunks):
+        rows = slice(CH * j, CH * (j + 1))
+        s = nn(kn[rows, :], q3t[...])
+        dp = nn(vn[rows, :], d3t[...])
+        t = biased(s, segk[rows, :] == segq[0], b1, b0, CH // BLOCK * j)
+        p = jnp.exp2(t - norm)
+        ds = (p * (dp - delta)).astype(BF16)
+        dv[rows, :] += nn(p.astype(BF16), d3[...])
+        dk[rows, :] += nn(ds, q3[...])
+        dq = dq + nn(kt[:, rows], ds)
+    heads = [dq[HEAD * h : HEAD * (h + 1), TILE * h : TILE * (h + 1)] for h in range(NH)]
+    merged = jnp.concatenate(heads, axis=0).T * HEAD ** (-0.5)
+    here = pl.ds(pl.multiple_of(step * TILE, TILE), TILE)
+    dqkv[here, : NH * HEAD] = merged.astype(BF16)
+
+    @pl.when(step == steps - 1)
+    def _():
+        gap = jnp.zeros((length, 256 - NH * HEAD), BF16)
+        for g in range(3):
+            dqkv[:, 256 * g + NH * HEAD : 256 * (g + 1)] = gap
+        dqkv[:, 256 : 256 + NH * HEAD] = (dk[...] * HEAD ** (-0.5)).astype(BF16)
+        dqkv[:, 512 : 512 + NH * HEAD] = dv[...].astype(BF16)
+
+
+def attend_backward(dat, qn, qt, otile, lse, b1, b0, segk, segq, kn, vn, kt):
+    length = kn.shape[0]
+    steps = length // TILE
+    blocks = length // BLOCK
+    whole = lambda *shape: pl.BlockSpec(shape, lambda i: (0,) * len(shape))
+    per = lambda *shape: pl.BlockSpec((1,) + shape, lambda i: (i,) + (0,) * len(shape))
+    return pl.pallas_call(
+        backward_kernel,
+        grid=(steps,),
+        in_specs=[
+            pl.BlockSpec((TILE, NH * HEAD), lambda i: (i, 0)),
+            pl.BlockSpec((TILE, 256), lambda i: (i, 0)),
+            pl.BlockSpec((256, TILE), lambda i: (0, i)),
+            per(NH * HEAD, TILE), per(1, NH * TILE),
+            per(blocks, NH * TILE), per(blocks, TILE),
+            whole(*segk.shape), per(1, TILE),
+            whole(*kn.shape), whole(*vn.shape), whole(*kt.shape),
+        ],
+        out_specs=whole(length, 768),
+        out_shape=jax.ShapeDtypeStruct((length, 768), BF16),
+        scratch_shapes=[
+            pltpu.VMEM((256, NH * TILE), BF16),
+            pltpu.VMEM((256, NH * TILE), BF16),
+            pltpu.VMEM((NH * TILE, NH * HEAD), BF16),
+            pltpu.VMEM((NH * TILE, NH * HEAD), BF16),
+            pltpu.VMEM((length, NH * HEAD), F32),
+            pltpu.VMEM((length, NH * HEAD), F32),
+        ],
+        name="attend_backward",
+    )(dat, qn, qt, otile, lse, b1, b0, segk, segq, kn, vn, kt)
+
+
+def tables(rand, seg):
+    blocks = rand.shape[0]
+    qb = jnp.arange(blocks, dtype=jnp.int32)
+    near = (jnp.abs(qb[:, None] - qb[None, :]) <= 1).astype(jnp.int32)
+    hits = jnp.sum((rand[:, None, :, :] == qb[None, :, None, None]).astype(jnp.int32), axis=3)
+    local = (qb >= 2).astype(jnp.int32)
+    listed = (near[:, :, None] + hits) * local[:, None, None]
+    fixed = ((qb[:, None] < 2) | (qb[None, :] < 2)).astype(jnp.int32)
+    log_of = lambda n: jnp.where(n > 0, jnp.log2(jnp.maximum(n, 1).astype(F32)), NEG)
+    b1 = log_of(listed + fixed[:, :, None])
+    b0 = log_of(fixed)
+    steps = blocks // 2
+    b1 = b1.reshape(steps, 2, blocks, NH).transpose(0, 2, 3, 1)
+    b1 = jnp.broadcast_to(b1[..., None], (steps, blocks, NH, 2, BLOCK)).reshape(steps, blocks, NH * TILE)
+    b0 = b0.reshape(steps, 2, blocks).transpose(0, 2, 1)
+    b0 = jnp.broadcast_to(b0[..., None], (steps, blocks, 2, BLOCK)).reshape(steps, blocks, TILE)
+    segk = jnp.broadcast_to(seg[:, None], (seg.shape[0], TILE))
+    segq = seg.reshape(steps, 1, TILE)
+    return b1, b0, segk, segq
+
+
+MESH = pl.DeviceIdType.MESH
+ANYSPACE = pl.BlockSpec(memory_space=pl.ANY)
+VMEMSPACE = pl.BlockSpec(memory_space=pltpu.VMEM)
+
+
+class Copies:
+    def __init__(self, send, recv):
+        self.send = send
+        self.recv = recv
+        self.used = 0
+
+    def to(self, src, dst, device):
+        index = self.used
+        self.used += 1
+        return pltpu.make_async_remote_copy(
+            src_ref=src, dst_ref=dst, send_sem=self.send.at[index], recv_sem=self.recv.at[index],
+            device_id=device, device_id_type=MESH,
+        )
+
+
+class Place:
+    def __init__(self):
+        self.d = lax.axis_index("dp")
+        self.t = lax.axis_index("seq")
+        self.x = lax.rem(self.d, 2)
+        self.y = self.d // 2
+        self.c = lax.rem(self.t, 2)
+        self.z = self.t // 2
+        self.half = self.z // 2
+        self.xn = self.d + 1 - 2 * self.x
+        self.yn = self.d + 2 - 4 * self.y
+        self.diag = 3 - self.d
+        self.pair_z = self.z + 1 - 2 * lax.rem(self.z, 2)
+        self.across_x = (self.xn, self.t)
+        self.across_y = (self.yn, self.t)
+        self.partner = (self.d, self.t + 1 - 2 * self.c)
+
+    def at_z(self, z):
+        return (self.d, 2 * z + self.c)
+
+
+def meet(devices):
+    barrier = pltpu.get_barrier_semaphore()
+    for device in devices:
+        pl.semaphore_signal(barrier, inc=1, device_id=device, device_id_type=MESH)
+    pl.semaphore_wait(barrier, len(devices))
+
+
+def gather_kernel(x, wg, wo, wu, wd, xs, wgf, wof, wuf, wdf, send, recv, xsend, xrecv, local):
+    me = Place()
+    d, t, c, z = me.d, me.t, me.c, me.z
+    mine, other = me.half, 1 - me.half
+    middle = 1 + me.half
+    is_middle = z == middle
+    z_step = [me.at_z(lax.rem(z + k, 4)) for k in (1, 2, 3)]
+    meet([me.across_x, me.across_y, me.partner] + z_step)
+    cps = Copies(send, recv)
+
+    wg_x = cps.to(wg, wgf.at[d], me.across_x)
+    wg_y = cps.to(wg, wgf.at[d], me.across_y)
+    wg_x.start()
+    wg_y.start()
+    near = cps.to(x.at[mine], xs.at[t], me.at_z(me.pair_z))
+    near.start()
+    row = lax.rem(z, 2)
+    far = pltpu.make_async_remote_copy(
+        src_ref=x.at[other], dst_ref=xs.at[t], send_sem=xsend.at[0], recv_sem=xrecv.at[row],
+        device_id=me.at_z(2 - me.half), device_id_type=MESH,
+    )
+    far.start()
+    give = cps.to(x.at[mine], xs.at[t], me.partner)
+    give.start()
+    keeps = [
+        pltpu.make_async_copy(x.at[mine], xs.at[t], local.at[0]),
+        pltpu.make_async_copy(wg, wgf.at[d], local.at[1]),
+        pltpu.make_async_copy(wo, wof.at[d], local.at[2]),
+        pltpu.make_async_copy(wu, wuf.at[d], local.at[3]),
+        pltpu.make_async_copy(wd, wdf.at[d], local.at[4]),
+    ]
+    for keep in keeps:
+        keep.start()
+    heavy = []
+    for w, full in ((wo, wof), (wu, wuf), (wd, wdf)):
+        rows = w.shape[0] // 2
+        part = pl.ds(pl.multiple_of(c * rows, rows), rows)
+        to_x = cps.to(w.at[part], full.at[d, part], me.across_x)
+        to_y = cps.to(w.at[part], full.at[d, part], me.across_y)
+        to_x.start()
+        to_y.start()
+        heavy.append((full, rows, to_x, to_y))
+
+    half = wg.shape[0] // 2
+    lo, hi = pl.ds(0, half), pl.ds(half, half)
+    wg_x.wait_recv()
+    wg_dy = cps.to(wgf.at[me.xn, lo], wgf.at[me.xn, lo], me.across_y)
+    wg_dy.start()
+    wg_y.wait_recv()
+    wg_dx = cps.to(wgf.at[me.yn, hi], wgf.at[me.yn, hi], me.across_x)
+    wg_dx.start()
+
+    near.wait_recv()
+    near_t = 2 * me.pair_z + c
+    pass_near = cps.to(xs.at[near_t], xs.at[near_t], me.partner)
+    pass_near.start()
+    passes = []
+    for j in range(2):
+        src_t = 2 * (2 * other + j) + c
+        relay = pltpu.make_async_remote_copy(
+            src_ref=xs.at[src_t], dst_ref=xs.at[src_t], send_sem=xsend.at[1 + j],
+            recv_sem=xrecv.at[j], device_id=me.at_z(me.pair_z), device_id_type=MESH,
+        )
+        relay.wait_recv()
+
+        @pl.when(is_middle)
+        def _():
+            relay.start()
+
+        onward = cps.to(xs.at[src_t], xs.at[src_t], me.partner)
+        onward.start()
+        passes.append((relay, onward))
+
+    tail = []
+    for full, rows, to_x, to_y in heavy:
+        part = pl.ds(pl.multiple_of(c * rows, rows), rows)
+        quarter = rows // 2
+        lo = pl.ds(pl.multiple_of(c * rows, quarter), quarter)
+        hi = pl.ds(pl.multiple_of(c * rows + quarter, quarter), quarter)
+        to_x.wait_recv()
+        dy = cps.to(full.at[me.xn, lo], full.at[me.xn, lo], me.across_y)
+        px = cps.to(full.at[me.xn, part], full.at[me.xn, part], me.partner)
+        dy.start()
+        px.start()
+        to_y.wait_recv()
+        dx = cps.to(full.at[me.yn, hi], full.at[me.yn, hi], me.across_x)
+        py = cps.to(full.at[me.yn, part], full.at[me.yn, part], me.partner)
+        dx.start()
+        py.start()
+        tail.append((full, part, lo, hi, dy, dx, px, py, to_x, to_y))
+    ends = []
+    for full, part, lo, hi, dy, dx, px, py, to_x, to_y in tail:
+        dy.wait_recv()
+        dx.wait_recv()
+        pd = cps.to(full.at[me.diag, part], full.at[me.diag, part], me.partner)
+        pd.start()
+        ends.append(pd)
+
+    wg_dy.wait_recv()
+    wg_dx.wait_recv()
+    give.wait_recv()
+    pass_near.wait_recv()
+    for relay, onward in passes:
+        onward.wait()
+
+        @pl.when(is_middle)
+        def _():
+            relay.wait_send()
+
+    for pd in ends:
+        pd.wait()
+    for full, part, lo, hi, dy, dx, px, py, to_x, to_y in tail:
+        px.wait()
+        py.wait()
+        for cp in (dy, dx, to_x, to_y):
+            cp.wait_send()
+    for cp in (wg_x, wg_y, wg_dx, wg_dy, near, far, give, pass_near):
+        cp.wait_send()
+    for keep in keeps:
+        keep.wait()
+
+
+def gather(x, wg, wo, wu, wd):
+    dp = lax.axis_size("dp")
+    seq = lax.axis_size("seq")
+    shapes = [(seq,) + x.shape[1:]] + [(dp,) + w.shape for w in (wg, wo, wu, wd)]
+    return pl.pallas_call(
+        gather_kernel,
+        in_specs=[VMEMSPACE] * 5,
+        out_specs=[ANYSPACE] * 5,
+        out_shape=[jax.ShapeDtypeStruct(shape, BF16) for shape in shapes],
+        scratch_shapes=[
+            pltpu.SemaphoreType.DMA((40,)),
+            pltpu.SemaphoreType.DMA((40,)),
+            pltpu.SemaphoreType.DMA((3,)),
+            pltpu.SemaphoreType.DMA((2,)),
+            pltpu.SemaphoreType.DMA((5,)),
+        ],
+        compiler_params=pltpu.CompilerParams(collective_id=0, has_side_effects=True),
+        name="gather",
+    )(x, wg, wo, wu, wd)
+
+
+def swap_kernel(src, dst, send, recv, local):
+    d = lax.axis_index("dp")
+    t = lax.axis_index("seq")
+    count = src.shape[0]
+    peers = [lax.rem(t + k, count) for k in range(1, count)]
+    meet([(d, peer) for peer in peers])
+    cps = Copies(send, recv)
+    moves = [cps.to(src.at[peer], dst.at[t], (d, peer)) for peer in peers]
+    for move in moves:
+        move.start()
+    keep = pltpu.make_async_copy(src.at[t], dst.at[t], local.at[0])
+    keep.start()
+    for move in moves:
+        move.wait()
+    keep.wait()
+
+
+def swap(src, number):
+    count = src.shape[0]
+    return pl.pallas_call(
+        swap_kernel,
+        in_specs=[VMEMSPACE],
+        out_specs=ANYSPACE,
+        out_shape=jax.ShapeDtypeStruct(src.shape, src.dtype),
+        scratch_shapes=[
+            pltpu.SemaphoreType.DMA((count,)),
+            pltpu.SemaphoreType.DMA((count,)),
+            pltpu.SemaphoreType.DMA((1,)),
+        ],
+        compiler_params=pltpu.CompilerParams(collective_id=number, has_side_effects=True),
+        name="swap",
+    )(src)
+
+
+def each(count, body):
+    def run(i, carry):
+        body(i)
+        return carry
+
+    lax.fori_loop(0, count, run, 0)
+
+
+def plus(a, b):
+    return a.astype(F32) + b.astype(F32)
+
+
+def reduce_kernel(*refs):
+    (g0, g1, g2, stats), refs = refs[:4], refs[4:]
+    (o0, o1, o2, stats_out), refs = refs[:4], refs[4:]
+    bufs, refs = refs[:18], refs[18:]
+    nsend, nrecv, send, recv, local = refs
+    me = Place()
+    c, z, x, y = me.c, me.z, me.x, me.y
+    z_step = [lax.rem(z + k, 4) for k in (1, 2, 3)]
+    meet([me.across_x, me.across_y, me.partner] + [me.at_z(k) for k in z_step])
+    cps = Copies(send, recv)
+    works = []
+    for i, (g, o) in enumerate(((g2, o2), (g1, o1), (g0, o0))):
+        own, ra, rb1, rb2, rc, rd = bufs[6 * i : 6 * i + 6]
+        swap_core = cps.to(g.at[:, :, :, 1 - c], ra, me.partner)
+        swap_core.start()
+        load = pltpu.make_async_copy(g.at[:, :, :, c], own, local.at[i])
+        load.start()
+        works.append((o, own, ra, rb1, rb2, rc, rd, swap_core, load))
+    stat_to = [me.partner, me.across_x, me.across_y, me.at_z(me.pair_z), me.at_z(lax.rem(z + 2, 4))]
+    nsend[0] = stats[...]
+    stat = cps.to(nsend.at[0], nrecv.at[0], stat_to[0])
+    stat.start()
+    stat_all = [stat]
+    stage_b = []
+    for o, own, ra, rb1, rb2, rc, rd, swap_core, load in works:
+        load.wait()
+        swap_core.wait_recv()
+
+        def fold(i):
+            yy, xx, zz = i // 8, lax.rem(i // 4, 2), lax.rem(i, 4)
+            own[yy, xx, zz] = plus(own[yy, xx, zz], ra[yy, xx, zz]).astype(BF16)
+
+        each(16, fold)
+        bx = cps.to(own.at[:, 1 - x, 0:2], rb1, me.across_x)
+        by = cps.to(own.at[1 - y, :, 2:4], rb2, me.across_y)
+        bx.start()
+        by.start()
+        stage_b.append((bx, by))
+        k = len(stat_all)
+        stat_all[-1].wait_recv()
+        nsend[k] = nsend[k - 1] + nrecv[k - 1]
+        stat = cps.to(nsend.at[k], nrecv.at[k], stat_to[k])
+        stat.start()
+        stat_all.append(stat)
+    stage_c = []
+    for (o, own, ra, rb1, rb2, rc, rd, swap_core, load), (bx, by) in zip(works, stage_b):
+        bx.wait_recv()
+
+        def fold_x(i):
+            yy, zz = i // 2, lax.rem(i, 2)
+            rb1[yy, zz] = plus(own[yy, x, zz], rb1[yy, zz]).astype(BF16)
+
+        each(4, fold_x)
+        cy = cps.to(rb1.at[1 - y], rc.at[0:2], me.across_y)
+        cy.start()
+        by.wait_recv()
+
+        def fold_y(i):
+            xx, zz = i // 2, lax.rem(i, 2)
+            rb2[xx, zz] = plus(own[y, xx, 2 + zz], rb2[xx, zz]).astype(BF16)
+
+        each(4, fold_y)
+        cx = cps.to(rb2.at[1 - x], rc.at[2:4], me.across_x)
+        cx.start()
+        stage_c.append((cy, cx))
+        if len(stat_all) < 5:
+            k = len(stat_all)
+            stat_all[-1].wait_recv()
+            nsend[k] = nsend[k - 1] + nrecv[k - 1]
+            stat = cps.to(nsend.at[k], nrecv.at[k], stat_to[k])
+            stat.start()
+            stat_all.append(stat)
+    stage_d = []
+    for (o, own, ra, rb1, rb2, rc, rd, swap_core, load), (cy, cx) in zip(works, stage_c):
+        cy.wait_recv()
+        cx.wait_recv()
+        for zz in range(2):
+            rc[zz] = plus(rb1[y, zz], rc[zz]).astype(BF16)
+            rc[2 + zz] = plus(rb2[x, zz], rc[2 + zz]).astype(BF16)
+        ds = [cps.to(rc.at[k], rd.at[j], me.at_z(k)) for j, k in enumerate(z_step)]
+        for cp in ds:
+            cp.start()
+        stage_d.append(ds)
+    stat_all[-1].wait_recv()
+    stats_out[...] = nsend[4] + nrecv[4]
+    for (o, own, ra, rb1, rb2, rc, rd, swap_core, load), ds in zip(works, stage_d):
+        for cp in ds:
+            cp.wait_recv()
+        o[...] = plus(rc[z], rd[0]) + plus(rd[1], rd[2])
+    for cp in stat_all:
+        cp.wait_send()
+    for work, bs, cs, ds in zip(works, stage_b, stage_c, stage_d):
+        for cp in (work[7],) + bs + cs + tuple(ds):
+            cp.wait_send()
+
+
+def reduce_grads(grads, stats):
+    dims = [g.shape[-2:] for g in grads]
+    bufs = []
+    for rows, cols in dims[::-1]:
+        bufs += [
+            pltpu.VMEM((2, 2, 4, rows, cols), BF16),
+            pltpu.VMEM((2, 2, 4, rows, cols), BF16),
+            pltpu.VMEM((2, 2, rows, cols), BF16),
+            pltpu.VMEM((2, 2, rows, cols), BF16),
+            pltpu.VMEM((4, rows, cols), BF16),
+            pltpu.VMEM((3, rows, cols), BF16),
+        ]
+    return pl.pallas_call(
+        reduce_kernel,
+        in_specs=[ANYSPACE] * 3 + [VMEMSPACE],
+        out_specs=[VMEMSPACE] * 4,
+        out_shape=[jax.ShapeDtypeStruct(dim, F32) for dim in dims]
+        + [jax.ShapeDtypeStruct(stats.shape, F32)],
+        scratch_shapes=bufs
+        + [
+            pltpu.VMEM((5,) + stats.shape, F32),
+            pltpu.VMEM((5,) + stats.shape, F32),
+            pltpu.SemaphoreType.DMA((29,)),
+            pltpu.SemaphoreType.DMA((29,)),
+            pltpu.SemaphoreType.DMA((3,)),
+        ],
+        compiler_params=pltpu.CompilerParams(collective_id=3, has_side_effects=True),
+        name="reduce_grads",
+    )(*grads, stats)
+
+
+def finish_kernel(
+    part, dwg, ig, wq, own, rp, ra, rb, ro, wb1, wb2, wc, wr, send, recv, local
+):
+    me = Place()
+    c, z, x, y, t = me.c, me.z, me.x, me.y, me.t
+    mine, other = me.half, 1 - me.half
+    is_middle = z == 1 + me.half
+    z_step = [lax.rem(z + k, 4) for k in (1, 2, 3)]
+    peers = [lax.rem(t + k, 8) for k in range(1, 8)]
+    meet([me.across_x, me.across_y] + [(me.d, peer) for peer in peers])
+    cps = Copies(send, recv)
+    core = cps.to(part.at[:, 1 - c], rp, me.partner)
+    core.start()
+    bx = cps.to(dwg.at[:, 1 - x, 0:4], wb1, me.across_x)
+    by = cps.to(dwg.at[1 - y, :, 4:8], wb2, me.across_y)
+    bx.start()
+    by.start()
+    core.wait_recv()
+
+    def fold(i):
+        own[i] = plus(part[i, c], rp[i]).astype(BF16)
+
+    each(4, fold)
+    near = cps.to(own.at[me.pair_z], ra, me.at_z(me.pair_z))
+    near.start()
+    middle_t = me.at_z(me.pair_z)
+    up = [cps.to(own.at[2 * other + j], rb.at[j], middle_t) for j in range(2)]
+    down = [
+        pltpu.make_async_remote_copy(
+            src_ref=own.at[2 * other + j], dst_ref=ro, send_sem=send.at[cps.used + j],
+            recv_sem=recv.at[cps.used], device_id=me.at_z(2 * other + j), device_id_type=MESH,
+        )
+        for j in range(2)
+    ]
+    cps.used += 2
+
+    @pl.when(z != 1 + me.half)
+    def _():
+        for cp in up:
+            cp.start()
+
+    bx.wait_recv()
+
+    def fold_x(i):
+        yy, tt = i // 4, lax.rem(i, 4)
+        wb1[yy, tt] = plus(dwg[yy, x, tt], wb1[yy, tt]).astype(BF16)
+
+    each(8, fold_x)
+    cy = cps.to(wb1.at[1 - y], wc.at[0:4], me.across_y)
+    cy.start()
+    by.wait_recv()
+
+    def fold_y(i):
+        xx, tt = i // 4, lax.rem(i, 4)
+        wb2[xx, tt] = plus(dwg[y, xx, 4 + tt], wb2[xx, tt]).astype(BF16)
+
+    each(8, fold_y)
+    cx = cps.to(wb2.at[1 - x], wc.at[4:8], me.across_x)
+    cx.start()
+
+    @pl.when(is_middle)
+    def _():
+        for j in range(2):
+            up[j].wait_recv()
+            own[2 * other + j] = plus(own[2 * other + j], rb[j]).astype(BF16)
+            down[j].start()
+
+    cy.wait_recv()
+    cx.wait_recv()
+
+    def fold_c(i):
+        wc[i] = plus(wb1[y, i], wc[i]).astype(BF16)
+        wc[4 + i] = plus(wb2[x, i], wc[4 + i]).astype(BF16)
+
+    each(4, fold_c)
+    moves = [cps.to(wc.at[peer], wr.at[t], (me.d, peer)) for peer in peers]
+    for move in moves:
+        move.start()
+    near.wait_recv()
+    ig[mine] = plus(own[z], ra[...])
+    down[0].wait_recv()
+    ig[other] = ro[...].astype(F32)
+    wr[t] = wc[t]
+    for move in moves:
+        move.wait_recv()
+    for g in range(4):
+        wq[g] = plus(wr[g], wr[4 + g])
+    for cp in [core, bx, by, near, cy, cx] + moves:
+        cp.wait_send()
+
+    @pl.when(z != 1 + me.half)
+    def _():
+        for cp in up:
+            cp.wait_send()
+
+    @pl.when(is_middle)
+    def _():
+        for cp in down:
+            cp.wait_send()
+
+
+def finish(part, dwg):
+    rows, cols = part.shape[-2:]
+    wrows, wcols = dwg.shape[-2:]
+    return pl.pallas_call(
+        finish_kernel,
+        in_specs=[VMEMSPACE] * 2,
+        out_specs=[VMEMSPACE] * 2,
+        out_shape=[
+            jax.ShapeDtypeStruct((2, rows, cols), F32),
+            jax.ShapeDtypeStruct((4, wrows, wcols), F32),
+        ],
+        scratch_shapes=[
+            pltpu.VMEM((4, rows, cols), BF16),
+            pltpu.VMEM((4, rows, cols), BF16),
+            pltpu.VMEM((rows, cols), BF16),
+            pltpu.VMEM((2, rows, cols), BF16),
+            pltpu.VMEM((rows, cols), BF16),
+            pltpu.VMEM((2, 4, wrows, wcols), BF16),
+            pltpu.VMEM((2, 4, wrows, wcols), BF16),
+            pltpu.VMEM((8, wrows, wcols), BF16),
+            pltpu.VMEM((8, wrows, wcols), BF16),
+            pltpu.SemaphoreType.DMA((20,)),
+            pltpu.SemaphoreType.DMA((20,)),
+            pltpu.SemaphoreType.DMA((1,)),
+        ],
+        compiler_params=pltpu.CompilerParams(collective_id=4, has_side_effects=True),
+        name="finish",
+    )(part, dwg)
+
+
+def head_layout(
+    inputs, segments, rand_blocks, w_qkv, w_out, w_up, w_down, norm_gain, norm_bias, out_grad
+):
+    seqs, tok, features = inputs.shape
+    seq = lax.axis_size("seq")
+    t = lax.axis_index("seq")
+    groups = seq // seqs
+    my_seq, my_group = t // groups, lax.rem(t, groups)
+    width = features // groups
+    shard = w_qkv.reshape(w_qkv.shape[0], 3, groups, width)
+    shard = lax.dynamic_index_in_dim(shard, my_group, 2, keepdims=False)
+    shard = jnp.pad(shard, ((0, 0), (0, 0), (0, 256 - width))).reshape(w_qkv.shape[0], 768)
+    rand = lax.dynamic_slice_in_dim(
+        lax.dynamic_index_in_dim(rand_blocks, my_seq, 0, keepdims=False), my_group * NH, NH, 1
+    )
+    seg = lax.dynamic_index_in_dim(segments, my_seq, 0, keepdims=False)
+    b1, b0, segk, segq = tables(rand, seg)
+    xs, wgf, wof, wuf, wdf = gather(inputs, shard, w_out, w_up, w_down)
+    xs = xs.reshape(seq * tok, features)
+    wgf = wgf.reshape(features, 768)
+    full_out = wof.reshape(features, features)
+    full_up = wuf.reshape(features, -1)
+    full_down = wdf.reshape(-1, features)
+    att, otile, lse, qn, kn, vn, qt, kt = attend_forward(xs, wgf, b1, b0, segk, segq)
+    att_home = swap(att.reshape(seq, tok, width), 1)
+    att_flat = (
+        att_home.reshape(seqs, groups, tok, width).transpose(0, 2, 1, 3).reshape(seqs * tok, features)
+    )
+    tokens_flat = inputs.reshape(seqs * tok, features)
+    resid_one = tokens_flat.astype(F32) + product(att_flat, full_out)
+    hidden_one, normed_one, inv_one = norm_forward(resid_one, norm_gain[0], norm_bias[0])
+    hidden_low = hidden_one.astype(BF16)
+    pre_act = product(hidden_low, full_up)
+    activated = gelu_value(pre_act).astype(BF16)
+    resid_two = hidden_one + product(activated, full_down)
+    result, normed_two, inv_two = norm_forward(resid_two, norm_gain[1], norm_bias[1])
+    grad_rows = out_grad.reshape(seqs * tok, features).astype(F32)
+    grad_resid_two, gain_two, shift_two = norm_backward(
+        grad_rows, normed_two, inv_two, norm_gain[1]
+    )
+    grad_branch = grad_resid_two.astype(BF16)
+    grad_down_w = product_tn(activated, grad_branch).astype(BF16)
+    grad_pre = (product_nt(grad_branch, full_down) * gelu_slope(pre_act)).astype(BF16)
+    grad_up_w = product_tn(hidden_low, grad_pre).astype(BF16)
+    grad_hidden = grad_resid_two + product_nt(grad_pre, full_up)
+    grad_resid_one, gain_one, shift_one = norm_backward(
+        grad_hidden, normed_one, inv_one, norm_gain[0]
+    )
+    grad_mix = grad_resid_one.astype(BF16)
+    grad_out_w = product_tn(att_flat, grad_mix).astype(BF16)
+    grad_att = product_nt(grad_mix, full_out).astype(BF16)
+    grad_att = grad_att.reshape(seqs, tok, groups, width).transpose(0, 2, 1, 3)
+    dat = swap(grad_att.reshape(seq, tok, width), 2).reshape(seq * tok, width)
+    stats = jnp.stack([gain_one, gain_two, shift_one, shift_two])
+    cut = lambda g: g.reshape(2, 2, 4, 2, g.shape[0] // 32, g.shape[1])
+    out_sum, up_sum, down_sum, stats = reduce_grads(
+        [cut(grad_out_w), cut(grad_up_w), cut(grad_down_w)], stats
+    )
+    dqkv = attend_backward(dat, qn, qt, otile, lse, b1, b0, segk, segq, kn, vn, kt)
+    part = product_nt(dqkv, wgf).astype(BF16).reshape(4, 2, tok, features)
+    dwg = product_tn(xs, dqkv).astype(BF16).reshape(2, 2, 8, features // 32, 768)
+    ig, wq = finish(part, dwg)
+    wq = wq.reshape(groups, features // 32, 3, 256)[..., :width].transpose(1, 2, 0, 3)
+    mine = lax.axis_index("dp") * seq + t
+    stats = lax.dynamic_slice_in_dim(stats, mine * (features // 32), features // 32, 1)
+    return (
+        result.astype(BF16).reshape(seqs, tok, features),
+        ig + grad_resid_one.reshape(seqs, tok, features),
+        wq.reshape(features // 32, 3 * features),
+        out_sum,
+        up_sum,
+        down_sum,
+        stats[:2],
+        stats[2:],
+    )
+
+
 def solution(mesh):
     in_specs = (
         P("dp", "seq", None),
@@ -529,6 +1328,7 @@
         P(None, ("dp", "seq")),
         P(None, ("dp", "seq")),
     )
+    fits = mesh.shape["dp"] == 4 and mesh.shape["seq"] == 8
     return jax.shard_map(
-        per_device, mesh=mesh, in_specs=in_specs, out_specs=out_specs, check_vma=False
-    )
+        head_layout if fits else per_device, mesh=mesh, in_specs=in_specs, out_specs=out_specs, check_vma=False
+    )

time: 1240 us -> 358 us (0.29)
  waiting for transfers between devices: 345 us -> 0 us
  local copies, waits for them, and re-layouts: 340 us -> 29.1 us
  Pallas kernels: 0 us -> 285 us
  blocking collectives: 180 us -> 0 us
  other arithmetic: 173 us -> 7.78 us
  matrix products: 135 us -> 33.5 us
  starting transfers between devices: 39 us -> 0 us
  between operations: 17 us -> 1.07 us
    pallas_call x0 -> x7, Pallas kernels: none -> 285 us  [the longest x1 79.5 us: reduce_grads(): pl.pallas_call(reduce_kernel, in_specs=[ANYSPACE] * 3 + [VMEMSPACE], out_...]
    reduce_scatter x3 -> x0, waiting for transfers between devices: 133 us -> none  [the longest x1 133 us: per_device(): lax.psum_scatter(grad_up_w, ('dp', 'seq'), scatter_dimension=0, tiled=True)]
    unnamed x12 -> x0, waiting for transfers between devices: 127 us -> none
    reshape x36 -> x10, local copies, waits for them, and re-layouts: 95.5 us -> 14.2 us  [the longest x2 5.04 us: head_layout(): grad_att = grad_att.reshape(seqs, tok, groups, width).transpose(0, 2, 1, 3)]
    all_gather x4 -> x0, blocking collectives: 78.3 us -> none  [merged(): everything = jax.tree.map(lambda part: lax.all_gather(part, axis), x)]
    dot_general x36 -> x0, matrix products: 71.3 us -> none  [the longest x2 9.08 us: per_device(): jnp.einsum('sbqhd,sbhkd->sbhqk', grad_local, random_vals, preferred_eleme...]
    psum x2 -> x0, blocking collectives: 61.5 us -> none  [the longest x1 35 us: per_device(): glob_out = lax.psum(glob_part, 'seq')]
    slice x28 -> x2, local copies, waits for them, and re-layouts: 59.4 us -> 1.38 us  [the longest x1 0.81 us: head_layout(): norm_bias[1]]
  transfers between devices with their start and end apart: 23 -> 0, of which waited for: 5 -> 0; matrix products, arithmetic and copies ran while one was open for 42% -> 0% of each run, Pallas kernels for 0% -> 0%
where the time goes in v1:
time: 358 us; the launch traced here: 357 us
  Pallas kernels  285 us (80%)
  matrix products  33.5 us (9%)
  local copies, waits for them, and re-layouts  29.1 us (8%)
  other arithmetic  7.78 us (2%)
    pallas_call x1, Pallas kernels, reduce_grads(): pl.pallas_call(reduce_kernel, in_specs=[ANYSPACE] * 3 + [VMEMSPACE], out_...  79.5 us
    pallas_call x1, Pallas kernels, gather(): pl.pallas_call(gather_kernel, in_specs=[VMEMSPACE] * 5, out_specs=[ANYSPA...  64.1 us
    pallas_call x1, Pallas kernels, finish(): pl.pallas_call(finish_kernel, in_specs=[VMEMSPACE] * 2, out_specs=[VMEMSP...  45.8 us
    pallas_call x2, Pallas kernels, swap(): pl.pallas_call(swap_kernel, in_specs=[VMEMSPACE], out_specs=ANYSPACE, out...  37.5 us
    pallas_call x1, Pallas kernels, attend_backward(): pl.pallas_call(backward_kernel, grid=(steps,), in_specs=[pl.BlockSpec((TI...  33.8 us
    pallas_call x1, Pallas kernels, attend_forward(): pl.pallas_call(forward_kernel, grid=(steps,), in_specs=[whole(*xs.shape),...  24.5 us
    dot_general x4, matrix products, product_tn(): lax.dot_general(left_side, right_side, (((0,), (0,)), ((), ())), preferre...  16.5 us
    dot_general x4, matrix products, product_nt(): lax.dot_general(left_side, right_side, (((1,), (1,)), ((), ())), preferre...  10.5 us

profile of v1, /device:TPU:0, one launch (start us, length us, event | category | flops | bytes accessed | tf_op | source)
XLA Modules:
  0.0 356.7 jit_solution(15123736039280680594)
XLA Ops:
  0.7 0.7 copy-done
  1.4 1.3 dynamic-slice_bitcast_fusion
  2.8 0.8 slice_reduce_fusion
  3.6 1.4 convert_reduce_fusion
  5.5 0.4 broadcast_in_dim.21
  5.9 0.9 reshape.244.b0
  7.1 1.1 broadcast_in_dim.19
  8.2 1.4 reshape.243.b1
  9.6 1.2 broadcast_in_dim.23.segk
  10.7 1.1 reshape.239
  11.8 0.6 constant_dynamic-slice_fusion.2
  13.0 0.8 copy.40
  13.7 64.1 %gather.1 = (bf16[8,192,768]{2,1,0:T(8,128)(2,1)}, bf16[4,192,768]{2,1,0:T(8,128)(2,1)}, bf16[4,192,768]{2,1,0:T(8,128)(2,1)}, bf16[4,192,3072]{2,1,0:T(8,128)(2,1)}, bf16[4,768,768]{2,1,0:T(8,128)(2,1)}) custom-call(bf16[2,192,768]{2,1,0:T(8,128)(2,1)} %x.3, bf16[192,768]{1,0:T(8,128)(2,1)} %bitcast.85, bf16[192,768]{1,0:T(8,128)(2,1)} %wo.1, ...), custom_call_target="tpu_custom_call" | custom-call | tf_op jit(solution)/shard_map/gather/pallas_call | solution.py:910
  77.8 24.5 %attend_forward.1 = (bf16[1536,192]{1,0:T(8,128)(2,1)}, f32[12,192,128]{2,1,0:T(8,128)}, f32[12,1,384]{2,1,0:T(1,128)}, bf16[1536,256]{1,0:T(8,128)(2,1)}, bf16[...) custom-call(bf16[1536,768]{1,0:T(8,128)(2,1)} %bitcast.81, ...), custom_call_target="tpu_custom_call" | custom-call | tf_op jit(solution)/shard_map/attend_forward/pallas_call | solution.py:601
  102.3 16.5 %swap.2 = bf16[8,192,192]{2,1,0:T(8,128)(2,1)} custom-call(bf16[8,192,192]{2,1,0:T(8,128)(2,1)} %bitcast.89), custom_call_target="tpu_custom_call" | custom-call | tf_op jit(solution)/shard_map/swap/pallas_call | solution.py:946
  118.7 1.8 copy.44
  120.6 0.7 reshape.248
  121.3 1.9 fusion.28
  123.8 2.4 multiply_convert_fusion
  126.3 2.2 fusion.29
  128.8 0.8 copy-done.2
  129.5 0.6 fusion.12
  130.1 1.3 fusion.9
  131.4 3.2 fusion.5
  134.6 2.4 multiply_reduce_fusion
  137.0 0.4 subtract_multiply_fusion
  137.4 0.9 copy-done.4
  138.3 1.5 convolution_convert_fusion.5
  139.8 0.6 pad_maximum_fusion.refs_3_
  140.4 2.9 reshape.253
  143.3 2.1 copy.36
  145.5 21.1 %swap.3 = bf16[8,192,192]{2,1,0:T(8,128)(2,1)} custom-call(bf16[8,192,192]{2,1,0:T(8,128)(2,1)} %bitcast.76), custom_call_target="tpu_custom_call" | custom-call | tf_op jit(solution)/shard_map/swap/pallas_call | solution.py:946
  166.5 33.8 %attend_backward.1 = bf16[1536,768]{1,0:T(8,128)(2,1)} custom-call(bf16[1536,192]{1,0:T(8,128)(2,1)} %bitcast.78, bf16[1536,256]{1,0:T(8,128)(2,1)} %get-tuple-element.33.qn, bf16[256,1536]{1,0:T(8,128)(2,1)} %get-tuple-element.34.qt, f32[12,192,128]{2,1,0:T(8,128)} %get-tuple-element.35.otile, f32[12,1,384]{2,1,0:T(1,128)} %get-tuple-element.36.lse, ...), custom_call_target="tpu_custom_call" | custom-call | tf_op jit(solution)/shard_map/attend_backward/pallas_call | solution.py:689
  200.4 5.6 %convolution_convert_fusion.4 = bf16[768,768]{1,0:T(8,128)(2,1)} fusion(bf16[1536,768]{1,0:T(8,128)(2,1)} %bitcast.82, bf16[1536,768]{1,0:T(8,128)(2,1)} %attend_backward.1), kind=kOutput, calls=%fused_computation.13 | convolution fusion | flops 1812529152 | bytes 5898240 | tf_op jit(solution)/shard_map/dot_general | solution.py:59
  206.0 3.5 convolution_convert_fusion.2
  209.5 45.8 %finish.1 = (f32[2,192,768]{2,1,0:T(8,128)}, f32[4,24,768]{2,1,0:T(8,128)}) custom-call(bf16[4,2,192,768]{3,2,1,0:T(8,128)(2,1)} %bitcast.79, bf16[2,2,8,24,768]{4,3,2,1,0:T(8,128)(2,1)} %bitcast.84), custom_call_target="tpu_custom_call" | custom-call | tf_op jit(solution)/shard_map/finish/pallas_call | solution.py:1204
  255.3 2.5 add.123
  257.8 1.1 reshape.259
  259.2 0.9 reshape.260
  260.1 1.8 convolution_convert_fusion.3
  261.9 4.7 %convolution_convert_fusion.1 = bf16[768,3072]{1,0:T(8,128)(2,1)} fusion(bf16[384,3072]{1,0:T(8,128)(2,1)S(1)} %copy-done.14, f32[384,768]{1,0:T(8,128)S(1)} %get-tuple-element.65, f32[768]{0:T(1024)S(1)} %get-tuple-element.57, f32[768]{0:T(1024)S(1)} %get-tuple-element.73, f32[384]{0:T(512)S(1)} %add_rsqrt_fusion.1, f32[384]{0:T(512)S(1)} %broadcast_multiply_fusion.5), kind=kOutput, calls=%fused_computation.2 | convolution fusion | flops 1815773184 | bytes 8266752 | tf_op jit(solution)/shard_map/dot_general | solution.py:59
  266.6 4.4 %convolution_convert_fusion = bf16[3072,768]{1,0:T(8,128)(2,1)} fusion(bf16[384,3072]{1,0:T(8,128)(2,1)S(1)} %copy-done.12, f32[384,768]{1,0:T(8,128)S(1)} %copy-done.7), kind=kOutput, calls=%fused_computation.1 | convolution fusion | flops 1814593536 | bytes 8257536 | tf_op jit(solution)/shard_map/dot_general | solution.py:59
  270.9 79.5 %reduce_grads.1 = (f32[24,768]{1,0:T(8,128)}, f32[24,3072]{1,0:T(8,128)}, f32[96,768]{1,0:T(8,128)}, f32[4,768]{1,0:T(4,128)}) custom-call(bf16[2,2,4,2,24,768]{5,4,3,2,1,0:T(8,128)(2,1)} %bitcast.74, bf16[2,2,4,2,24,3072]{5,4,3,2,1,0:T(8,128)(2,1)} %bitcast.72, bf16[2,2,4,2,96,768]{5,4,3,2,1,0:T(8,128)(2,1)} %bitcast.73, f32[4,768]{1,0:T(4,128)} %pad_maximum_fusion.refs_3_), custom_call_target="tpu_custom_call" | custom-call | tf_op jit(solution)/shard_map/reduce_grads/pallas_call | solution.py:1081
  350.4 0.8 constant_dynamic-slice_fusion
  351.2 0.6 fusion.27
  351.8 1.5 copy.50
  353.3 1.7 copy.51
  355.0 1.7 copy.52
  (63 shorter events, 2.6 us)
Async XLA Ops:
  0.6 0.8 copy-start
  8.2 2.6 copy-start.9
  118.7 2.6 copy-start.3
  121.3 2.5 copy-start.10
  123.2 3.0 slice-start
  123.8 2.5 slice-start.1
  126.3 2.2 copy-start.11
  128.5 1.1 copy-start.2
  131.4 3.2 copy-start.6
  134.6 2.4 copy-start.13
  137.0 1.3 copy-start.4
  200.4 5.6 %copy-start.5 = (bf16[1536,768]{1,0:T(8,128)(2,1)S(1)}, bf16[1536,768]{1,0:T(8,128)(2,1)}, u32[]{:S(2)}) copy-start(bf16[1536,768]{1,0:T(8,128)(2,1)} %attend_backward.1) | copy-start | bytes 7077892
  200.4 5.6 %copy-start.8 = (bf16[4,192,768]{2,1,0:T(8,128)(2,1)S(1)}, bf16[4,192,768]{2,1,0:T(8,128)(2,1)}, u32[]{:S(2)}) copy-start(bf16[4,192,768]{2,1,0:T(8,128)(2,1)} %get-tuple-element.28) | copy-start | bytes 3538948
  260.0 1.8 copy-start.14
  261.9 4.7 %copy-start.7 = (f32[384,768]{1,0:T(8,128)S(1)}, f32[384,768]{1,0:T(8,128)}, u32[]{:S(2)}) copy-start(f32[384,768]{1,0:T(8,128)} %copy-done.6) | copy-start | bytes 3538948
  261.9 4.7 %copy-start.12 = (bf16[384,3072]{1,0:T(8,128)(2,1)S(1)}, bf16[384,3072]{1,0:T(8,128)(2,1)}, u32[]{:S(2)}) copy-start(bf16[384,3072]{1,0:T(8,128)(2,1)} %copy-done.11) | copy-start | bytes 7077892
  270.9 85.8 %copy-start.1 = (s32[2,24,12,3]{1,0,3,2:T(2,128)S(1)}, s32[2,24,12,3]{1,0,3,2:T(2,128)}, u32[]{:S(2)}) copy-start(s32[2,24,12,3]{1,0,3,2:T(2,128)} %param.12) | copy-start | bytes 20740
